TPU v7x, 32 devices: a whole 2x2x4 slice. The times are simulated.
32 devices in a mesh: dp: 32 (over z, y, x, core).
Axes of the slice: x: 2, y: 2, z: 4, core: 2. Of those that a mesh axis runs over, the one named last changes fastest.
Arguments:
- tokens: bfloat16 [2, 32, 256, 768], P(None, None, 'dp'), may hold values from -6 to 6
- lengths: int32 [2, 32], replicated, may hold values from 1 to 256, 5120 in all within a row
- order: int32 [2, 32], replicated, may hold values from 0 to 31, each once within a row
- weight_in: bfloat16 [768, 2304], P('dp'), may hold values from -0.3125 to 0.3125
- bias_in: bfloat16 [1536], P('dp'), may hold values from -1.5 to 1.5
- weight_mix: bfloat16 [768, 768], P('dp'), may hold values from -1.25 to 1.25
- bias_mix: bfloat16 [768], P('dp'), may hold values from -1.5 to 1.5
- gain_first: bfloat16 [768], P('dp'), may hold values from 0.25 to 1.75
- shift_first: bfloat16 [768], P('dp'), may hold values from -1.5 to 1.5
- weight_up: bfloat16 [768, 3072], P('dp'), may hold values from -0.21875 to 0.21875
- bias_up: bfloat16 [3072], P('dp'), may hold values from -1.5 to 1.5
- weight_down: bfloat16 [3072, 768], P('dp'), may hold values from -0.15625 to 0.15625
- bias_down: bfloat16 [768], P('dp'), may hold values from -1.5 to 1.5
- gain_second: bfloat16 [768], P('dp'), may hold values from 0.25 to 1.75
- shift_second: bfloat16 [768], P('dp'), may hold values from -1.5 to 1.5
- cotangent: bfloat16 [2, 32, 256, 768], P(None, None, 'dp'), may hold values from -6 to 6
Outputs:
- layer_out: bfloat16 [2, 32, 256, 768], P(None, None, 'dp')
- tokens_grad: bfloat16 [2, 32, 256, 768], P(None, None, 'dp')
- weight_in_grad: float32 [768, 2304], P('dp')
- bias_in_grad: float32 [1536], P('dp')
- weight_mix_grad: float32 [768, 768], P('dp')
- bias_mix_grad: float32 [768], P('dp')
- gain_first_grad: float32 [768], P('dp')
- shift_first_grad: float32 [768], P('dp')
- weight_up_grad: float32 [768, 3072], P('dp')
- bias_up_grad: float32 [3072], P('dp')
- weight_down_grad: float32 [3072, 768], P('dp')
- bias_down_grad: float32 [768], P('dp')
- gain_second_grad: float32 [768], P('dp')
- shift_second_grad: float32 [768], P('dp')
Inputs may be any that keep to these rules, and one draw needn't show every extreme that they name: In each micro-batch the 32 lengths sum to 5120, and the longest is exactly 256. Each row of order names every input sequence of its micro-batch exactly once.
All inputs are finite; a program needn't handle non-finite values.
Results may differ from a plain program's by a relative error of at most 0.015.
The roundings to bfloat16 on the way count: a program that leaves them out, or rounds other values in their place, can miss the bound.
Values may be sent and summed in bfloat16 or wider, within the bound.
A program may use at most 128 MiB of HBM per device.

v0:
```python
import jax
import jax.numpy as jnp
from jax import lax
from jax.sharding import PartitionSpec as P

HD = 64


epsilon = 1e-12


def matmul(left, right):
    return jnp.dot(left, right, preferred_element_type=jnp.float32)


def rows_product(left, right):
    return lax.dot_general(
        left, right, (((0,), (0,)), ((), ())), preferred_element_type=jnp.float32
    )


def right_transposed(left, right):
    return lax.dot_general(
        left, right, (((1,), (1,)), ((), ())), preferred_element_type=jnp.float32
    )


def split_heads(block, heads):
    return block.reshape(block.shape[0], heads, -1).transpose(1, 0, 2)


def join_heads(block):
    return block.transpose(1, 0, 2).reshape(block.shape[1], -1)


def norm_forward(summed, norm_gain, norm_shift):
    row_mean = jnp.mean(summed, -1, keepdims=True)
    centered = summed - row_mean
    reciprocal = lax.rsqrt(jnp.mean(centered * centered, -1, keepdims=True) + epsilon)
    normed = centered * reciprocal
    return (normed * norm_gain + norm_shift, normed, reciprocal)


def norm_backward(upstream, normed, reciprocal, norm_gain):
    scaled = upstream * norm_gain
    summed_grad = reciprocal * (
        scaled
        - jnp.mean(scaled, -1, keepdims=True)
        - normed * jnp.mean(scaled * normed, -1, keepdims=True)
    )
    return (summed_grad, jnp.sum(upstream * normed, 0), jnp.sum(upstream, 0))


def head_scores(head_query, head_keys, valid):
    scores = right_transposed(head_query, head_keys) * 0.125
    return jnp.where(valid[None, :], scores, -1e30)


def attend_forward(packed, valid):
    head_query, head_keys, head_values = packed
    scores = head_scores(head_query, head_keys, valid)
    row_max = jnp.max(scores, -1, keepdims=True)
    weights_raw = jnp.exp(scores - row_max)
    row_sum = jnp.sum(weights_raw, -1, keepdims=True)
    probability = weights_raw / row_sum
    context = matmul(probability.astype(jnp.bfloat16), head_values)
    return (context, (row_max + jnp.log(row_sum))[:, 0])


def attend_backward(packed, valid):
    head_query, head_keys, head_values, context_grad, log_total = packed
    scores = head_scores(head_query, head_keys, valid)
    probability = jnp.exp(scores - log_total[:, None])
    low_prob = probability.astype(jnp.bfloat16)
    prob_grad = right_transposed(context_grad, head_values)
    value_grad = rows_product(low_prob, context_grad)
    shifted = prob_grad - jnp.sum(probability * prob_grad, -1, keepdims=True)
    score_grad = (probability * shifted).astype(jnp.bfloat16)
    query_grad = matmul(score_grad, head_keys) * 0.125
    key_grad = rows_product(score_grad, head_query) * 0.125
    return (query_grad, key_grad, value_grad)


def forward(weights, sequence, length):
    (
        weight_in,
        bias_in,
        weight_mix,
        bias_mix,
        gain_first,
        shift_first,
        weight_up,
        bias_up,
        weight_down,
        bias_down,
        gain_second,
        shift_second,
    ) = weights
    width = sequence.shape[1]
    heads = width // HD
    valid = jnp.arange(sequence.shape[0], dtype=jnp.int32) < length
    bias_full = jnp.concatenate(
        [
            bias_in[:width].astype(jnp.float32),
            jnp.zeros((width,), jnp.float32),
            bias_in[width:].astype(jnp.float32),
        ]
    )
    projected = (matmul(sequence, weight_in) + bias_full).astype(jnp.bfloat16)
    queries = split_heads(projected[:, :width], heads)
    key_heads = split_heads(projected[:, width : 2 * width], heads)
    value_heads = split_heads(projected[:, 2 * width :], heads)
    context, log_total = lax.map(
        lambda packed: attend_forward(packed, valid), (queries, key_heads, value_heads)
    )
    context_low = join_heads(context).astype(jnp.bfloat16)
    branch = matmul(context_low, weight_mix) + bias_mix.astype(jnp.float32)
    hidden, normed_first, recip_first = norm_forward(
        sequence.astype(jnp.float32) + branch,
        gain_first.astype(jnp.float32),
        shift_first.astype(jnp.float32),
    )
    hidden_low = hidden.astype(jnp.bfloat16)
    preact = matmul(hidden_low, weight_up) + bias_up.astype(jnp.float32)
    activated = jax.nn.gelu(preact, approximate=False).astype(jnp.bfloat16)
    feed_out = matmul(activated, weight_down) + bias_down.astype(jnp.float32)
    result, normed_second, recip_second = norm_forward(
        hidden + feed_out, gain_second.astype(jnp.float32), shift_second.astype(jnp.float32)
    )
    stored = (
        valid,
        queries,
        key_heads,
        value_heads,
        log_total,
        context_low,
        normed_first,
        recip_first,
        hidden_low,
        preact,
        activated,
        normed_second,
        recip_second,
    )
    return (result.astype(jnp.bfloat16), stored)


def backward(weights, sequence, upstream_low, stored):
    (
        weight_in,
        bias_in,
        weight_mix,
        bias_mix,
        gain_first,
        shift_first,
        weight_up,
        bias_up,
        weight_down,
        bias_down,
        gain_second,
        shift_second,
    ) = weights
    (
        valid,
        queries,
        key_heads,
        value_heads,
        log_total,
        context_low,
        normed_first,
        recip_first,
        hidden_low,
        preact,
        activated,
        normed_second,
        recip_second,
    ) = stored
    width = sequence.shape[1]
    heads = width // HD
    upstream = upstream_low.astype(jnp.float32)
    second_grad, gain_second_grad, shift_second_grad = norm_backward(
        upstream, normed_second, recip_second, gain_second.astype(jnp.float32)
    )
    feed_grad = second_grad.astype(jnp.bfloat16)
    bias_down_grad = jnp.sum(feed_grad.astype(jnp.float32), 0)
    weight_down_grad = rows_product(activated, feed_grad)
    act_grad = right_transposed(feed_grad, weight_down)
    slope = (
        0.5 * (1.0 + jax.scipy.special.erf(preact * 0.7071067811865476))
        + preact * jnp.exp(-0.5 * preact * preact) * 0.3989422804014327
    )
    preact_grad = (act_grad * slope).astype(jnp.bfloat16)
    bias_up_grad = jnp.sum(preact_grad.astype(jnp.float32), 0)
    weight_up_grad = rows_product(hidden_low, preact_grad)
    hidden_grad = second_grad + right_transposed(preact_grad, weight_up)
    first_grad, gain_first_grad, shift_first_grad = norm_backward(
        hidden_grad, normed_first, recip_first, gain_first.astype(jnp.float32)
    )
    branch_grad = first_grad.astype(jnp.bfloat16)
    bias_mix_grad = jnp.sum(branch_grad.astype(jnp.float32), 0)
    weight_mix_grad = rows_product(context_low, branch_grad)
    context_grad = right_transposed(branch_grad, weight_mix).astype(jnp.bfloat16)
    query_grad, key_grad, value_grad = lax.map(
        lambda packed: attend_backward(packed, valid),
        (queries, key_heads, value_heads, split_heads(context_grad, heads), log_total),
    )
    projected_grad = jnp.concatenate(
        [join_heads(query_grad), join_heads(key_grad), join_heads(value_grad)], -1
    ).astype(jnp.bfloat16)
    column_sums = jnp.sum(projected_grad.astype(jnp.float32), 0)
    bias_in_grad = jnp.concatenate([column_sums[:width], column_sums[2 * width :]])
    weight_in_grad = rows_product(sequence, projected_grad)
    input_grad = (first_grad + right_transposed(projected_grad, weight_in)).astype(jnp.bfloat16)
    gradients = (
        weight_in_grad,
        bias_in_grad,
        weight_mix_grad,
        bias_mix_grad,
        gain_first_grad,
        shift_first_grad,
        weight_up_grad,
        bias_up_grad,
        weight_down_grad,
        bias_down_grad,
        gain_second_grad,
        shift_second_grad,
    )
    return (input_grad, gradients)


def fetch_weights(shards):
    return (
        lax.all_gather(shards[0], "dp", axis=0, tiled=True),
        lax.all_gather(shards[1], "dp", axis=0, tiled=True),
        lax.all_gather(shards[2], "dp", axis=0, tiled=True),
        lax.all_gather(shards[3], "dp", axis=0, tiled=True),
        lax.all_gather(shards[4], "dp", axis=0, tiled=True),
        lax.all_gather(shards[5], "dp", axis=0, tiled=True),
        lax.all_gather(shards[6], "dp", axis=0, tiled=True),
        lax.all_gather(shards[7], "dp", axis=0, tiled=True),
        lax.all_gather(shards[8], "dp", axis=0, tiled=True),
        lax.all_gather(shards[9], "dp", axis=0, tiled=True),
        lax.all_gather(shards[10], "dp", axis=0, tiled=True),
        lax.all_gather(shards[11], "dp", axis=0, tiled=True),
    )


def add_trees(first, second):
    if first is None:
        return second
    return jax.tree.map(lambda left, right: left + right, first, second)


def local(
    tokens,
    lengths,
    order,
    weight_in,
    bias_in,
    weight_mix,
    bias_mix,
    gain_first,
    shift_first,
    weight_up,
    bias_up,
    weight_down,
    bias_down,
    gain_second,
    shift_second,
    cotangent,
):
    shards = (
        weight_in,
        bias_in,
        weight_mix,
        bias_mix,
        gain_first,
        shift_first,
        weight_up,
        bias_up,
        weight_down,
        bias_down,
        gain_second,
        shift_second,
    )
    device = lax.axis_index("dp")
    totals = None
    outputs_list = []
    grads_list = []
    for batch in range(tokens.shape[0]):
        current = fetch_weights(shards)
        picks = order[batch]
        dealt_tokens = tokens[batch][picks]
        sequence, upstream = (
            lax.all_to_all(dealt_tokens, "dp", split_axis=0, concat_axis=1, tiled=True),
            lax.all_to_all(cotangent[batch], "dp", split_axis=0, concat_axis=1, tiled=True),
        )
        length = lengths[batch][picks[device]]
        result, stored = forward(current, sequence[0], length)
        behind = (
            lax.all_gather(shards[0], "dp", axis=0, tiled=True),
            lax.all_gather(shards[1], "dp", axis=0, tiled=True),
            lax.all_gather(shards[2], "dp", axis=0, tiled=True),
            lax.all_gather(shards[3], "dp", axis=0, tiled=True),
            lax.all_gather(shards[4], "dp", axis=0, tiled=True),
            lax.all_gather(shards[5], "dp", axis=0, tiled=True),
            lax.all_gather(shards[6], "dp", axis=0, tiled=True),
            lax.all_gather(shards[7], "dp", axis=0, tiled=True),
            lax.all_gather(shards[8], "dp", axis=0, tiled=True),
            lax.all_gather(shards[9], "dp", axis=0, tiled=True),
            lax.all_gather(shards[10], "dp", axis=0, tiled=True),
            lax.all_gather(shards[11], "dp", axis=0, tiled=True),
        )
        input_grad, gradients = backward(behind, sequence[0], upstream[0], stored)
        back_out, back_grad = (
            lax.all_to_all(result[None], "dp", split_axis=1, concat_axis=0, tiled=True),
            lax.all_to_all(input_grad[None], "dp", split_axis=1, concat_axis=0, tiled=True),
        )
        restored = jnp.zeros_like(back_grad).at[picks].set(back_grad)
        outputs_list.append(back_out)
        grads_list.append(restored)
        totals = add_trees(totals, gradients)
    totals = (
        lax.psum_scatter(totals[0], "dp", scatter_dimension=0, tiled=True),
        lax.psum_scatter(totals[1], "dp", scatter_dimension=0, tiled=True),
        lax.psum_scatter(totals[2], "dp", scatter_dimension=0, tiled=True),
        lax.psum_scatter(totals[3], "dp", scatter_dimension=0, tiled=True),
        lax.psum_scatter(totals[4], "dp", scatter_dimension=0, tiled=True),
        lax.psum_scatter(totals[5], "dp", scatter_dimension=0, tiled=True),
        lax.psum_scatter(totals[6], "dp", scatter_dimension=0, tiled=True),
        lax.psum_scatter(totals[7], "dp", scatter_dimension=0, tiled=True),
        lax.psum_scatter(totals[8], "dp", scatter_dimension=0, tiled=True),
        lax.psum_scatter(totals[9], "dp", scatter_dimension=0, tiled=True),
        lax.psum_scatter(totals[10], "dp", scatter_dimension=0, tiled=True),
        lax.psum_scatter(totals[11], "dp", scatter_dimension=0, tiled=True),
    )
    return (
        jnp.stack(outputs_list),
        jnp.stack(grads_list),
        totals[0],
        totals[1],
        totals[2],
        totals[3],
        totals[4],
        totals[5],
        totals[6],
        totals[7],
        totals[8],
        totals[9],
        totals[10],
        totals[11],
    )


def solution(mesh):
    return jax.shard_map(
        local,
        mesh=mesh,
        in_specs=(
            P(None, None, "dp", None),
            P(),
            P(),
            P("dp", None),
            P("dp"),
            P("dp", None),
            P("dp"),
            P("dp"),
            P("dp"),
            P("dp", None),
            P("dp"),
            P("dp", None),
            P("dp"),
            P("dp"),
            P("dp"),
            P(None, None, "dp", None),
        ),
        out_specs=(
            P(None, None, "dp", None),
            P(None, None, "dp", None),
            P("dp", None),
            P("dp"),
            P("dp", None),
            P("dp"),
            P("dp"),
            P("dp"),
            P("dp", None),
            P("dp"),
            P("dp", None),
            P("dp"),
            P("dp"),
            P("dp"),
        ),
        check_vma=False,
    )
```

profile of v0, /device:TPU:0, one launch (start us, length us, event | category | flops | bytes accessed | tf_op | source)
XLA Modules:
  0.0 936.7 jit_solution(8899604694317877735)
XLA Ops:
  11.6 7.3 all-to-all-start.4
  20.3 13.5 %all-to-all-done.4 = bf16[32,8,768]{2,1,0:T(8,128)(2,1)S(1)} async-done(((bf16[32,8,768]{2,1,0:T(8,128)(2,1)}), bf16[32,8,768]{2,1,0:T(8,128)(2,1)S(1)}, u32[]{:S(2)}, u32[]{:S(2)}) %all-to-all-start.4) | async-done | bytes 393248 | tf_op jit(solution)/shard_map/all_to_all | solution.py:296
  37.8 15.3 %all-to-all-done.6 = bf16[32,8,768]{2,1,0:T(8,128)(2,1)S(1)} async-done(((bf16[32,8,768]{2,1,0:T(8,128)(2,1)}), bf16[32,8,768]{2,1,0:T(8,128)(2,1)S(1)}, u32[]{:S(2)}, u32[]{:S(2)}) %all-to-all-start.6) | async-done | bytes 393248 | tf_op jit(solution)/shard_map/all_to_all | solution.py:296
  61.6 40.9 %all-reduce.17 = (bf16[3072]{0:T(1024)(128)(2,1)S(1)}, bf16[1536]{0:T(1024)(128)(2,1)S(1)}, bf16[768]{0:T(1024)(128)(2,1)S(1)}, bf16[768]{0:T(1024)(128)(2,1)S(1...) all-reduce(bf16[3072]{0:T(1024)(128)(2,1)S(1)} %dynamic-update-slic, ...), channel_id=1, replica_groups=mesh['dp'=32] {'dp'}, use_global_device_ids=true, to_apply=%add.4 | all-reduce | flops 9216 | bytes 36864
  110.3 4.5 all-to-all-start.2
  127.0 40.0 %while.56 = (s32[]{:T(128)}, bf16[12,256,64]{1,2,0:T(8,128)(2,1)S(1)}, f32[12,256]{1,0:T(8,128)}, bf16[12,256,64]{2,1,0:T(8,128)(2,1)S(1)}, bf16[12,256,64]{2,1,...) while((s32[]{:T(128)}, ...), condition=%wide.region_3.4_spmd.clone, body=%wide.region_0.3_spmd.clone.sunk | while | flops 17301504 | bytes 1061741 | solution.py:113
  181.0 35.7 %while.57 = (s32[]{:T(128)}, bf16[12,256,64]{1,2,0:T(8,128)(2,1)S(1)}, f32[12,256]{1,0:T(8,128)S(1)}, bf16[12,256,64]{2,1,0:T(8,128)(2,1)}, bf16[12,256,64]{2,1,...) while((s32[]{:T(128)}, ...), condition=%wide.region_11.12_spmd.clone, body=%wide.region_8.11_spmd.clone.sunk | while | flops 17301504 | bytes 1061485 | solution.py:113
  220.6 11.3 %fusion.98 = (bf16[256,3072]{1,0:T(8,128)(2,1)}, f32[256,3072]{1,0:T(8,128)}) fusion(f32[3072]{0:T(1024)} %convert_element_type.195, bf16[768,3072]{1,0:T(8,128)(2,1)} %all-gather.9.cloned.1.call-done, f32[256,768]{1,0:T(8,128)S(1)} %get-tuple-element.542, f32[768]{0:T(1024)S(1)} %convert_element_type.193, f32[768]{0:T(1024)S(1)} %convert_element_type.192, ...), kind=kOutput, calls=%fused_computation.139 | convolution fusion | flops 1260847104 | bytes 10244096 | tf_op jit(solution)/shard_map/dot_general | solution.py:13
  231.9 35.4 %all-gather.11.cloned.1.call-done = bf16[3072,768]{1,0:T(8,128)(2,1)} async-done(((bf16[96,768]{1,0:T(8,128)(2,1)}), bf16[3072,768]{1,0:T(8,128)(2,1)}) %all-gather.11.cloned.1.call-update) | async-done | bytes 4718608 | tf_op jit(solution)/shard_map/all_gather | solution.py:241
  267.3 4.5 fusion.187
  272.1 8.0 fusion.101
  303.6 100.5 %while.59 = (s32[]{:T(128)}, bf16[12,256,64]{1,2,0:T(8,128)(2,1)}, bf16[12,256,64]{1,2,0:T(8,128)(2,1)}, bf16[12,256,64]{1,2,0:T(8,128)(2,1)}, bf16[12,256,64]{2...) while((s32[]{:T(128)}, bf16[12,256,64]{1,2,0:T(8,128)(2,1)}, ...), condition=%wide.region_30.31_spmd.clone, body=%wide.region_28.30_spmd.clone.sunk | while | flops 42565632 | bytes 2566781 | solution.py:203
  415.2 86.4 %while.58 = (s32[]{:T(128)}, bf16[12,256,64]{1,2,0:T(8,128)(2,1)S(1)}, bf16[12,256,64]{1,2,0:T(8,128)(2,1)S(1)}, bf16[12,256,64]{1,2,0:T(8,128)(2,1)}, bf16[12,2...) while((s32[]{:T(128)}, ...), condition=%wide.region_22.23_spmd.clone, body=%wide.region_20.22_spmd.clone.sunk | while | flops 42565632 | bytes 2566781 | solution.py:203
  503.9 4.0 convolution_add_fusion
  511.8 5.2 convolution_add_fusion.2
  520.3 5.2 convolution_add_fusion.1
  527.7 3.8 reduce.14
  538.8 3.8 reduce.15
  544.4 5.9 all-to-all-done.3
  558.4 4.0 reduce.16
  579.3 11.6 %all-to-all-done.7 = bf16[32,2,3072]{2,1,0:T(2,128)(2,1)S(1)} async-done(((bf16[32,2,3072]{2,1,0:T(2,128)(2,1)}), bf16[32,2,3072]{2,1,0:T(2,128)(2,1)S(1)}, u32[]{:S(2)}, u32[]{:S(2)}) %all-to-all-start.7) | async-done | bytes 393248 | tf_op jit(solution)/shard_map/all_to_all | solution.py:317
  598.8 41.9 %all-reduce.16 = (f32[1536]{0:T(1024)S(1)}, f32[768]{0:T(1024)S(1)}, f32[768]{0:T(1024)S(1)}, f32[768]{0:T(1024)S(1)}, f32[3072]{0:T(1024)S(1)}, /*index=5*/f32[...) all-reduce(f32[1536]{0:T(1024)S(1)} %maximum_add_fusion, ...), channel_id=3, replica_groups=mesh['dp'=32] {'dp'}, use_global_device_ids=true, to_apply=%region_35.36.clone | all-reduce | flops 9216 | bytes 73728
  656.9 130.6 %reduce-scatter.9.cloned.1.call-done = f32[24,3072]{1,0:T(8,128)} async-done(((f32[768,3072]{1,0:T(8,128)}), f32[24,3072]{1,0:T(8,128)}) %reduce-scatter.9.cloned.1.call-update) | async-done | bytes 294928 | tf_op jit(solution)/shard_map/reduce_scatter | solution.py:330
  787.5 142.1 %reduce-scatter.11.cloned.1.call-done = f32[96,768]{1,0:T(8,128)} async-done(((f32[3072,768]{1,0:T(8,128)}), f32[96,768]{1,0:T(8,128)}) %reduce-scatter.11.cloned.1.call-update) | async-done | bytes 294928 | tf_op jit(solution)/shard_map/reduce_scatter | solution.py:332
  (653 shorter events, 416.9 us)
Async XLA Ops:
  7.2 108.2 %all-gather.5.cloned.1.call-start = ((), (), s32[]{:S(2)}) async-start(), calls=%async_computation.12 | async-start | bytes 3649536 | tf_op jit(solution)/shard_map/all_gather | solution.py:233
  7.9 159.1 %all-gather.7.cloned.1.call-start = ((), (), s32[]{:S(2)}) async-start(), calls=%async_computation.13 | async-start | bytes 1216512 | tf_op jit(solution)/shard_map/all_gather | solution.py:235
  8.7 211.9 %all-gather.9.cloned.1.call-start = ((), (), s32[]{:S(2)}) async-start(), calls=%async_computation.14 | async-start | bytes 4866048 | tf_op jit(solution)/shard_map/all_gather | solution.py:239
  9.5 51.2 %copy-start.60 = (bf16[24]{0:T(256)(128)(2,1)S(1)}, bf16[24]{0:T(256)(128)(2,1)}, u32[]{:S(2)}) copy-start(bf16[24]{0:T(256)(128)(2,1)} %param.38) | copy-start | bytes 148
  9.5 51.4 %copy-start.61 = (bf16[24]{0:T(256)(128)(2,1)S(1)}, bf16[24]{0:T(256)(128)(2,1)}, u32[]{:S(2)}) copy-start(bf16[24]{0:T(256)(128)(2,1)} %param.37) | copy-start | bytes 148
  9.5 51.6 %copy-start.62 = (bf16[96]{0:T(256)(128)(2,1)S(1)}, bf16[96]{0:T(256)(128)(2,1)}, u32[]{:S(2)}) copy-start(bf16[96]{0:T(256)(128)(2,1)} %param.34) | copy-start | bytes 580
  9.5 51.9 %copy-start.63 = (bf16[48]{0:T(256)(128)(2,1)S(1)}, bf16[48]{0:T(256)(128)(2,1)}, u32[]{:S(2)}) copy-start(bf16[48]{0:T(256)(128)(2,1)} %param.28) | copy-start | bytes 292
  11.6 22.2 %all-to-all-start.4 = ((bf16[32,8,768]{2,1,0:T(8,128)(2,1)}), bf16[32,8,768]{2,1,0:T(8,128)(2,1)S(1)}, u32[]{:S(2)}, u32[]{:S(2)}) async-start(bf16[32,8,768]{2,1,0:T(8,128)(2,1)} %get-tuple-element.514), calls=%async_computation.4 | async-start | bytes 786432 | tf_op jit(solution)/shard_map/all_to_all | solution.py:296
  18.9 248.4 %all-gather.11.cloned.1.call-start = ((), (), s32[]{:S(2)}) async-start(), calls=%async_computation.15 | async-start | bytes 4866048 | tf_op jit(solution)/shard_map/all_gather | solution.py:241
  20.2 90.0 %copy-start.47 = (s32[32]{0:T(128)}, s32[32]{0:T(128)S(1)}, u32[]{:S(2)}) copy-start(s32[32]{0:T(128)S(1)} %get-tuple-element.540) | copy-start | bytes 388
  33.8 19.3 %all-to-all-start.6 = ((bf16[32,8,768]{2,1,0:T(8,128)(2,1)}), bf16[32,8,768]{2,1,0:T(8,128)(2,1)S(1)}, u32[]{:S(2)}, u32[]{:S(2)}) async-start(bf16[32,8,768]{2,1,0:T(8,128)(2,1)} %get-tuple-element.515), calls=%async_computation.6 | async-start | bytes 786432 | tf_op jit(solution)/shard_map/all_to_all | solution.py:296
  53.1 57.2 %all-to-all-start = ((bf16[32,8,768]{2,1,0:T(8,128)(2,1)}), bf16[32,8,768]{2,1,0:T(8,128)(2,1)S(1)}, u32[]{:S(2)}, u32[]{:S(2)}) async-start(bf16[32,8,768]{2,1,0:T(8,128)(2,1)} %gather_fusion), calls=%async_computation | async-start | bytes 786432 | tf_op jit(solution)/shard_map/all_to_all | solution.py:295
  110.3 57.7 %copy-start.7 = (bf16[32,8,768]{2,1,0:T(8,128)(2,1)}, bf16[32,8,768]{2,1,0:T(8,128)(2,1)S(1)}, u32[]{:S(2)}) copy-start(bf16[32,8,768]{2,1,0:T(8,128)(2,1)S(1)} %all-to-all-done) | copy-start | bytes 1179652
  110.3 59.6 %all-to-all-start.2 = ((bf16[32,8,768]{2,1,0:T(8,128)(2,1)}), bf16[32,8,768]{2,1,0:T(8,128)(2,1)S(1)}, u32[]{:S(2)}, u32[]{:S(2)}) async-start(bf16[32,8,768]{2,1,0:T(8,128)(2,1)} %gather_fusion.1), calls=%async_computation.2 | async-start | bytes 786432 | tf_op jit(solution)/shard_map/all_to_all | solution.py:295
  114.8 542.1 %reduce-scatter.7.cloned.1.call-start = ((), (), s32[]{:S(2)}) async-start(), calls=%async_computation.17 | async-start | bytes 2433024 | tf_op jit(solution)/shard_map/reduce_scatter | solution.py:326
  414.3 242.7 %reduce-scatter.5.cloned.1.call-start = ((), (), s32[]{:S(2)}) async-start(), calls=%async_computation.16 | async-start | bytes 7299072 | tf_op jit(solution)/shard_map/reduce_scatter | solution.py:324
  415.2 86.4 %copy-start.8 = (bf16[32,8,768]{2,1,0:T(8,128)(2,1)S(1)}, bf16[32,8,768]{2,1,0:T(8,128)(2,1)}, u32[]{:S(2)}) copy-start(bf16[32,8,768]{2,1,0:T(8,128)(2,1)} %copy-done.7) | copy-start | bytes 1179652
  508.0 279.5 %reduce-scatter.9.cloned.1.call-start = ((), (), s32[]{:S(2)}) async-start(), calls=%async_computation.18 | async-start | bytes 9732096 | tf_op jit(solution)/shard_map/reduce_scatter | solution.py:330
  517.0 412.6 %reduce-scatter.11.cloned.1.call-start = ((), (), s32[]{:S(2)}) async-start(), calls=%async_computation.19 | async-start | bytes 9732096 | tf_op jit(solution)/shard_map/reduce_scatter | solution.py:332
  533.4 16.9 %all-to-all-start.3 = ((bf16[32,2,3072]{2,1,0:T(2,128)(2,1)}), bf16[32,2,3072]{2,1,0:T(2,128)(2,1)}, u32[]{:S(2)}, u32[]{:S(2)}) async-start(bf16[32,2,3072]{2,1,0:T(2,128)(2,1)} %reshape.416), calls=%async_computation.3 | async-start | bytes 786432 | tf_op jit(solution)/shard_map/all_to_all | solution.py:316
  550.3 16.5 %all-to-all-start.1 = ((bf16[32,2,3072]{2,1,0:T(2,128)(2,1)}), bf16[32,2,3072]{2,1,0:T(2,128)(2,1)}, u32[]{:S(2)}, u32[]{:S(2)}) async-start(bf16[32,2,3072]{2,1,0:T(2,128)(2,1)} %reshape.418), calls=%async_computation.1 | async-start | bytes 786432 | tf_op jit(solution)/shard_map/all_to_all | solution.py:316
  566.8 24.2 %all-to-all-start.7 = ((bf16[32,2,3072]{2,1,0:T(2,128)(2,1)}), bf16[32,2,3072]{2,1,0:T(2,128)(2,1)S(1)}, u32[]{:S(2)}, u32[]{:S(2)}) async-start(bf16[32,2,3072]{2,1,0:T(2,128)(2,1)} %reshape.420), calls=%async_computation.7 | async-start | bytes 786432 | tf_op jit(solution)/shard_map/all_to_all | solution.py:317
  590.9 53.9 %copy-start.24 = (bf16[32,2,3072]{2,1,0:T(2,128)(2,1)}, bf16[32,2,3072]{2,1,0:T(2,128)(2,1)S(1)}, u32[]{:S(2)}) copy-start(bf16[32,2,3072]{2,1,0:T(2,128)(2,1)S(1)} %all-to-all-done.7) | copy-start | bytes 1179652
  590.9 60.5 %all-to-all-start.5 = ((bf16[32,2,3072]{2,1,0:T(2,128)(2,1)}), bf16[32,2,3072]{2,1,0:T(2,128)(2,1)S(1)}, u32[]{:S(2)}, u32[]{:S(2)}) async-start(bf16[32,2,3072]{2,1,0:T(2,128)(2,1)} %reshape.422), calls=%async_computation.5 | async-start | bytes 786432 | tf_op jit(solution)/shard_map/all_to_all | solution.py:317
  (59 other events, 728.3 us)
Sparse Core Ops, SparseCore 0:
  10.9 68.1 all-gather.4
  82.0 54.4 all-gather.6
  139.4 62.5 all-gather.8
  204.8 62.4 all-gather.10
  414.4 97.9 reduce-scatter.6
  519.4 126.8 reduce-scatter.4
  652.8 134.6 reduce-scatter.8
  795.0 134.5 reduce-scatter.10
where the time goes:
time: 952 us; the launch traced here: 937 us
  waiting for transfers between devices  361 us (38%)
  matrix products  280 us (29%)
  local copies, waits for them, and re-layouts  94.2 us (10%)
  blocking collectives  82.8 us (9%)
  other arithmetic  66.8 us (7%)
  starting transfers between devices  31.8 us (3%)
  between operations  19.5 us (2%)
    reduce_scatter x1, waiting for transfers between devices, local(): lax.psum_scatter(totals[8], 'dp', scatter_dimension=0, tiled=True)  142 us
    reduce_scatter x1, waiting for transfers between devices, local(): lax.psum_scatter(totals[6], 'dp', scatter_dimension=0, tiled=True)  131 us
    dot_general x56, matrix products, rows_product(): lax.dot_general(left, right, (((0,), (0,)), ((), ())), preferred_element_...  99.4 us
    dot_general x56, matrix products, matmul(): return jnp.dot(left, right, preferred_element_type=jnp.float32)  92.6 us
    dot_general x80, matrix products, right_transposed(): lax.dot_general(left, right, (((1,), (1,)), ((), ())), preferred_element_...  87.5 us
    unnamed x2, blocking collectives  82.8 us
    all_gather x1, waiting for transfers between devices, fetch_weights(): lax.all_gather(shards[8], 'dp', axis=0, tiled=True)  35.4 us
    unnamed x177, local copies, waits for them, and re-layouts  31.6 us
  transfers between devices with their start and end apart: 16, of which 8 were waited for; matrix products, arithmetic and copies ran while one was open for 31% of the time, Pallas kernels for 0%

commit v1 on v0

--- a/solution.py
+++ b/solution.py
@@ -1,7 +1,14 @@
+import functools
+import types
+
 import jax
 import jax.numpy as jnp
 from jax import lax
+from jax.experimental import pallas as pl
+from jax.experimental.pallas import tpu as pltpu
 from jax.sharding import PartitionSpec as P
+
+MESH = pl.DeviceIdType.MESH
 
 HD = 64
 
@@ -228,6 +235,17 @@
     return (input_grad, gradients)
 
 
+def permuted(blocks, picks):
+    chosen = (picks[:, None] == jnp.arange(picks.shape[0])[None, :]).astype(blocks.dtype)
+    flat = blocks.reshape(blocks.shape[0], -1)
+    return matmul(chosen, flat).astype(blocks.dtype).reshape(blocks.shape)
+
+
+def inverse_of(picks):
+    slots = jnp.arange(picks.shape[0], dtype=jnp.int32)
+    return jnp.sum(jnp.where(picks[:, None] == slots[None, :], slots[:, None], 0), 0)
+
+
 def fetch_weights(shards):
     return (
         lax.all_gather(shards[0], "dp", axis=0, tiled=True),
@@ -251,7 +269,7 @@
     return jax.tree.map(lambda left, right: left + right, first, second)
 
 
-def local(
+def portable(
     tokens,
     lengths,
     order,
@@ -290,12 +308,12 @@
     for batch in range(tokens.shape[0]):
         current = fetch_weights(shards)
         picks = order[batch]
-        dealt_tokens = tokens[batch][picks]
+        dealt_tokens = permuted(tokens[batch], picks)
         sequence, upstream = (
             lax.all_to_all(dealt_tokens, "dp", split_axis=0, concat_axis=1, tiled=True),
             lax.all_to_all(cotangent[batch], "dp", split_axis=0, concat_axis=1, tiled=True),
         )
-        length = lengths[batch][picks[device]]
+        length = jnp.sum(jnp.where(jnp.arange(picks.shape[0]) == picks[device], lengths[batch], 0))
         result, stored = forward(current, sequence[0], length)
         behind = (
             lax.all_gather(shards[0], "dp", axis=0, tiled=True),
@@ -316,7 +334,7 @@
             lax.all_to_all(result[None], "dp", split_axis=1, concat_axis=0, tiled=True),
             lax.all_to_all(input_grad[None], "dp", split_axis=1, concat_axis=0, tiled=True),
         )
-        restored = jnp.zeros_like(back_grad).at[picks].set(back_grad)
+        restored = permuted(back_grad, inverse_of(picks))
         outputs_list.append(back_out)
         grads_list.append(restored)
         totals = add_trees(totals, gradients)
@@ -352,6 +370,966 @@
     )
 
 
+COUNT = 32
+ROWS, LAYERS = 8, 4
+
+
+def meet_all(me):
+    barrier = pltpu.get_barrier_semaphore()
+
+    def greet(step, carry):
+        pl.semaphore_signal(
+            barrier, inc=1, device_id=(lax.rem(me + step, COUNT),), device_id_type=MESH
+        )
+        return carry
+
+    lax.fori_loop(1, COUNT, greet, 0)
+    pl.semaphore_wait(barrier, COUNT - 1)
+
+
+def remote(source, target, send_sem, recv_sem, device):
+    return pltpu.make_async_remote_copy(
+        src_ref=source,
+        dst_ref=target,
+        send_sem=send_sem,
+        recv_sem=recv_sem,
+        device_id=(device,),
+        device_id_type=MESH,
+    )
+
+
+WIDTHS = (48, 24, 24, 24, 96, 24, 24, 24)
+BIAS_IN, BIAS_MIX, GAIN_FIRST, SHIFT_FIRST, BIAS_UP, BIAS_DOWN, GAIN_SECOND, SHIFT_SECOND = range(8)
+TILE = 256
+PAIR = 128
+
+
+def contract(left, right, left_dim, right_dim):
+    return lax.dot_general(
+        left,
+        right,
+        (((left_dim,), (right_dim,)), ((), ())),
+        preferred_element_type=jnp.float32,
+    )
+
+
+def owners(width):
+    lane = lax.broadcasted_iota(jnp.int32, (COUNT, COUNT * width), 1)
+    owner = (lane * (-(-(1 << 20) // width))) >> 20
+    device = lax.broadcasted_iota(jnp.int32, (COUNT, COUNT * width), 0)
+    return owner == device
+
+
+def places(width):
+    lane = lax.broadcasted_iota(jnp.int32, (PAIR, COUNT * width), 1)
+    owner = (lane * (-(-(1 << 20) // width))) >> 20
+    entry = lax.broadcasted_iota(jnp.int32, (PAIR, COUNT * width), 0)
+    return jnp.where(lane - owner * width == entry, 1.0, 0.0).astype(jnp.bfloat16)
+
+
+def columns(tile, size=TILE):
+    return pl.ds(pl.multiple_of(tile * size, size), size)
+
+
+def flat(value):
+    return value.reshape(-1, value.shape[-1])
+
+
+def take_rows(ref, start, stop):
+    layers, seats, groups, small, _ = ref.shape
+    pieces = []
+    while start < stop:
+        layer, rest = divmod(start // small, seats * groups)
+        seat, group = divmod(rest, groups)
+        whole = min((stop - start) // (small * groups), seats - seat)
+        if group == 0 and whole:
+            pieces.append(flat(ref[layer, seat : seat + whole]))
+            start += whole * groups * small
+        else:
+            end = min(groups, group + (stop - start) // small)
+            pieces.append(flat(ref[layer, seat, group:end]))
+            start += (end - group) * small
+    return jnp.concatenate(pieces, 0)
+
+
+class Layer:
+    def __init__(self, refs):
+        self.__dict__.update(refs)
+        self.rows, self.width = self.normed.shape
+        self.hidden_width = self.slope.shape[1]
+
+    def spread_small(self):
+        for place, width in enumerate(WIDTHS):
+            given = self.small[:, place, :].astype(jnp.bfloat16)
+            spread = contract(given, places(width), 1, 0)
+            row = jnp.sum(jnp.where(owners(width), spread, 0.0), 0, keepdims=True)
+            if place == BIAS_IN:
+                self.bias_row[:, : self.width] = row[:, : self.width]
+                self.bias_row[:, self.width : 2 * self.width] = jnp.zeros_like(row[:, : self.width])
+                self.bias_row[:, 2 * self.width :] = row[:, self.width :]
+            elif place == BIAS_UP:
+                self.up_row[...] = row
+            else:
+                self.vectors[place : place + 1, :] = row
+
+    def vector(self, place):
+        return self.vectors[place : place + 1, :]
+
+    def project(self, tile):
+        here = columns(tile)
+        value = jnp.dot(
+            flat(self.sequence[...]),
+            flat(self.weight_in[:, :, :, :, here]),
+            preferred_element_type=jnp.float32
+        )
+        value = (value + self.bias_row[:, here]).astype(jnp.bfloat16)
+        scale = jnp.where(tile < self.width // TILE, 0.125, 1.0).astype(jnp.bfloat16)
+        self.packed[:, here] = value * scale
+
+    def heads_of(self, step):
+        pairs = self.width // PAIR
+        batch, pair = step // pairs, step % pairs
+        rows = pl.ds(pl.multiple_of(batch * TILE, TILE), TILE)
+        return batch, pair, rows
+
+    def block(self, part, rows, pair):
+        offset = pl.multiple_of(part * self.width + pair * PAIR, PAIR)
+        return self.packed[rows, pl.ds(offset, PAIR)]
+
+    def half(self, value, head):
+        lane = lax.broadcasted_iota(jnp.int32, value.shape, 1)
+        keep = lane < PAIR // 2 if head == 0 else lane >= PAIR // 2
+        return jnp.where(keep, value, jnp.zeros_like(value))
+
+    def attend(self, step):
+        batch, pair, rows = self.heads_of(step)
+        queries, key_block, value_block = (self.block(part, rows, pair) for part in range(3))
+        length = jnp.where(batch == 0, self.lengths[0], self.lengths[1])
+        lane = lax.broadcasted_iota(jnp.int32, (1, TILE), 1)
+        blocked = jnp.where(lane < length, 0.0, -1e30)
+        context = []
+        for head in range(2):
+            scores = contract(self.half(queries, head), key_block, 1, 1) + blocked
+            weights = jnp.exp(scores - jnp.max(scores, -1, keepdims=True))
+            total = jnp.sum(weights, -1, keepdims=True)
+            low = (weights * (1.0 / total)).astype(jnp.bfloat16)
+            self.chances[2 * step + head] = low
+            context.append(jnp.dot(low, value_block, preferred_element_type=jnp.float32))
+        lane = lax.broadcasted_iota(jnp.int32, context[0].shape, 1)
+        joined = jnp.where(lane < PAIR // 2, context[0], context[1])
+        self.context[rows, columns(pair, PAIR)] = joined.astype(jnp.bfloat16)
+
+    def mix(self, part):
+        rows = columns(part)
+        branch = jnp.dot(
+            self.context[rows, :], flat(self.weight_mix[...]), preferred_element_type=jnp.float32
+        )
+        summed = flat(self.sequence[part]).astype(jnp.float32) + (branch + self.vector(BIAS_MIX))
+        centered = summed - jnp.mean(summed, -1, keepdims=True)
+        factor = lax.rsqrt(jnp.mean(centered * centered, -1, keepdims=True) + epsilon)
+        normed = centered * factor
+        hidden = normed * self.vector(GAIN_FIRST) + self.vector(SHIFT_FIRST)
+        self.normed[rows, :] = normed
+        self.factor[rows, :] = factor
+        self.hidden_low[rows, :] = hidden.astype(jnp.bfloat16)
+
+    def up(self, tile):
+        here = columns(tile)
+        value = jnp.dot(
+            self.hidden_low[...], flat(self.weight_up[:, :, :, :, here]), preferred_element_type=jnp.float32
+        )
+        value = value + self.up_row[:, here]
+        below = 0.5 * (1.0 + lax.erf(value * 0.7071067811865476))
+        density = jnp.exp(-0.5 * value * value) * 0.3989422804014327
+        self.active[:, here] = (value * below).astype(jnp.bfloat16)
+        self.slope[:, here] = (below + value * density).astype(self.slope.dtype)
+
+    def down(self, tile):
+        here = columns(tile)
+        self.upper[:, here] = jnp.dot(
+            self.active[...], flat(self.weight_down[:, :, :, :, here]), preferred_element_type=jnp.float32
+        )
+
+    def finish(self, part, size=128):
+        rows = columns(part, size)
+        hidden = self.normed[rows, :] * self.vector(GAIN_FIRST) + self.vector(SHIFT_FIRST)
+        summed = hidden + (self.upper[rows, :] + self.vector(BIAS_DOWN))
+        centered = summed - jnp.mean(summed, -1, keepdims=True)
+        factor = lax.rsqrt(jnp.mean(centered * centered, -1, keepdims=True) + epsilon)
+        normed = centered * factor
+        gain = self.vector(GAIN_SECOND)
+        low = (normed * gain + self.vector(SHIFT_SECOND)).astype(jnp.bfloat16)
+        parts, seats = TILE // size, size // 8
+        batch, span = part // parts, pl.ds((part % parts) * seats, seats)
+        self.result[batch, span] = low.reshape(seats, 8, self.width)
+        upstream = flat(self.upstream[batch, span]).astype(jnp.float32)
+        grad = self.norm_backward(upstream, normed, factor, gain, GAIN_SECOND, SHIFT_SECOND)
+        low = grad.astype(jnp.bfloat16)
+        self.upper[rows, :] = grad
+        self.feed_grad[rows, :] = low
+        self.add_term(BIAS_DOWN, low.astype(jnp.float32))
+
+    def add_term(self, place, value):
+        self.terms[place : place + 1, :] += jnp.sum(value, 0, keepdims=True)
+
+    def norm_backward(self, upstream, normed, factor, gain, gain_place, shift_place):
+        self.add_term(gain_place, upstream * normed)
+        self.add_term(shift_place, upstream)
+        scaled = upstream * gain
+        return factor * (
+            scaled
+            - jnp.mean(scaled, -1, keepdims=True)
+            - normed * jnp.mean(scaled * normed, -1, keepdims=True)
+        )
+
+    def down_weight_grad(self, layer):
+        span = self.hidden_width // LAYERS
+        made = [
+            contract(self.active[:, columns(layer * (span // TILE) + i)], self.feed_grad[...], 0, 0)
+            for i in range(span // TILE)
+        ]
+        made = jnp.concatenate([part.astype(jnp.bfloat16) for part in made], 0)
+        self.down_grad[layer] = made.reshape(self.down_grad.shape[1:])
+
+    def active_backward(self, layer):
+        span = self.hidden_width // LAYERS
+        weight = flat(self.weight_down[layer])
+        for i in range(span // TILE):
+            here = columns(layer * (span // TILE) + i)
+            grad = contract(self.feed_grad[...], weight[i * TILE : (i + 1) * TILE], 1, 1)
+            low = (grad * self.slope[:, here].astype(jnp.float32)).astype(jnp.bfloat16)
+            self.preact_grad[:, here] = low
+            self.up_terms[:, here] = jnp.sum(low.astype(jnp.float32), 0, keepdims=True)
+
+    def up_weight_grad(self, tile):
+        here = columns(tile)
+        grad = contract(self.hidden_low[...], self.preact_grad[:, here], 0, 0)
+        self.keep_columns(self.up_grad, here, grad)
+
+    def hidden_backward(self, tile):
+        here = columns(tile)
+        weight = take_rows(self.weight_up, tile * TILE, (tile + 1) * TILE)
+        self.upper[:, here] += contract(self.preact_grad[...], weight, 1, 1)
+
+    def first_backward(self, part, size=128):
+        rows = columns(part, size)
+        grad = self.norm_backward(
+            self.upper[rows, :],
+            self.normed[rows, :],
+            self.factor[rows, :],
+            self.vector(GAIN_FIRST),
+            GAIN_FIRST,
+            SHIFT_FIRST,
+        )
+        low = grad.astype(jnp.bfloat16)
+        self.upper[rows, :] = grad
+        self.feed_grad[rows, :] = low
+        self.add_term(BIAS_MIX, low.astype(jnp.float32))
+
+    def mix_weight_grad(self, tile):
+        here = columns(tile)
+        grad = contract(self.context[...], self.feed_grad[:, here], 0, 0)
+        self.keep_columns(self.mix_grad, here, grad)
+
+    def mix_backward(self, tile):
+        here = columns(tile)
+        weight = take_rows(self.weight_mix, tile * TILE, (tile + 1) * TILE)
+        self.context_grad[:, here] = contract(self.feed_grad[...], weight, 1, 1).astype(
+            jnp.bfloat16
+        )
+
+    def attend_backward(self, step):
+        batch, pair, rows = self.heads_of(step)
+        queries, key_block, value_block = (self.block(part, rows, pair) for part in range(3))
+        grads = self.context_grad[rows, columns(pair, PAIR)]
+        query_grad = key_grad = value_grad = 0.0
+        for head in range(2):
+            low = self.chances[2 * step + head]
+            chance = low.astype(jnp.float32)
+            mine = self.half(grads, head)
+            chance_grad = contract(mine, value_block, 1, 1)
+            moved = chance_grad - jnp.sum(chance * chance_grad, -1, keepdims=True)
+            score_grad = (chance * moved).astype(jnp.bfloat16)
+            value_grad += contract(low, mine, 0, 0)
+            query_grad += jnp.dot(
+                score_grad, self.half(key_block, head), preferred_element_type=jnp.float32
+            )
+            key_grad += contract(score_grad, self.half(queries, head), 0, 0)
+        for part, grad in enumerate((query_grad * 0.125, key_grad, value_grad)):
+            offset = pl.multiple_of(part * self.width + pair * PAIR, PAIR)
+            self.packed[rows, pl.ds(offset, PAIR)] = grad.astype(jnp.bfloat16)
+
+    def in_weight_grad(self, tile):
+        here = columns(tile)
+        grads = self.packed[:, here]
+        self.keep_columns(self.in_grad, here, contract(flat(self.sequence[...]), grads, 0, 0))
+        self.in_terms[:, here] = jnp.sum(grads.astype(jnp.float32), 0, keepdims=True)
+
+    def input_backward(self, tile):
+        here = columns(tile)
+        weight = take_rows(self.weight_in, tile * TILE, (tile + 1) * TILE)
+        grad = self.upper[:, here] + contract(self.packed[...], weight, 1, 1)
+        shape = self.input_grad.shape[:3] + (TILE,)
+        self.input_grad[:, :, :, here] = grad.astype(jnp.bfloat16).reshape(shape)
+
+    def keep_columns(self, ref, here, grad):
+        ref[:, :, :, :, here] = grad.astype(jnp.bfloat16).reshape(ref.shape[:4] + (TILE,))
+
+    def gather_terms(self):
+        for place, width in enumerate(WIDTHS):
+            if place == BIAS_IN:
+                row = jnp.concatenate(
+                    [self.in_terms[:, : self.width], self.in_terms[:, 2 * self.width :]], -1
+                )
+            elif place == BIAS_UP:
+                row = self.up_terms[...]
+            else:
+                row = self.terms[place : place + 1, :]
+            high = row.astype(jnp.bfloat16)
+            rest = row - high.astype(jnp.float32)
+            middle = rest.astype(jnp.bfloat16)
+            low = (rest - middle.astype(jnp.float32)).astype(jnp.bfloat16)
+            keep, spots = owners(width), places(width)
+            self.small_grad[:, place, :] = sum(
+                contract(jnp.where(keep, part.astype(jnp.float32), 0.0).astype(jnp.bfloat16), spots, 1, 1)
+                for part in (high, middle, low)
+            )
+
+
+def scratch_of(rows, width, hidden_width):
+    low, full = jnp.bfloat16, jnp.float32
+    return dict(
+        bias_row=pltpu.VMEM((1, 3 * width), full),
+        up_row=pltpu.VMEM((1, hidden_width), full),
+        vectors=pltpu.VMEM((8, width), full),
+        terms=pltpu.VMEM((8, width), full),
+        up_terms=pltpu.VMEM((1, hidden_width), full),
+        in_terms=pltpu.VMEM((1, 3 * width), full),
+        packed=pltpu.VMEM((rows, 3 * width), low),
+        chances=pltpu.VMEM((2 * rows // TILE * width // PAIR, TILE, TILE), low),
+        context=pltpu.VMEM((rows, width), low),
+        normed=pltpu.VMEM((rows, width), full),
+        factor=pltpu.VMEM((rows, 1), full),
+        hidden_low=pltpu.VMEM((rows, width), low),
+        active=pltpu.VMEM((rows, hidden_width), low),
+        slope=pltpu.VMEM((rows, hidden_width), low),
+        upper=pltpu.VMEM((rows, width), full),
+        feed_grad=pltpu.VMEM((rows, width), low),
+    )
+
+
+class Spot:
+    def __init__(self):
+        self.me = me = lax.axis_index("dp")
+        core, column, row = me % 2, (me // 2) % 2, (me // 4) % 2
+        self.layer, self.seat = me // 8, me % 8
+        self.to_sibling = 1 - 2 * core
+        across_row = 4 * (1 - 2 * row)
+        across_column = 2 * (1 - 2 * column)
+        self.to_second = (1 - core) * across_row + core * across_column
+        self.to_third = (1 - core) * across_column + core * across_row
+        self.sibling = me + self.to_sibling
+        self.second = me + self.to_second
+        self.third = me + self.to_third
+        self.above = [lax.rem(self.layer + step, LAYERS) for step in (1, 2, 3)]
+
+
+class Chunk:
+    def __init__(self, kind, groups, cols):
+        self.kind, self.groups, self.cols = kind, groups, cols
+
+    def line(self, refs, seat):
+        return refs[self.kind].at[:, seat, self.groups, :, self.cols]
+
+    def block(self, refs, layer, seat):
+        return refs[self.kind].at[layer, seat, self.groups, :, self.cols]
+
+    def bulk(self, refs, layers, lines):
+        return refs[self.kind].at[pl.ds(0, layers), pl.ds(0, lines), self.groups, :, self.cols]
+
+
+def chunks_of(shapes):
+    made = []
+    for kind, (groups, _, width) in enumerate(shapes):
+        if kind < 3:
+            size = shapes[1][2]
+            for start in range(0, width, size):
+                made.append(Chunk(kind, pl.ds(0, groups), pl.ds(start, size)))
+        else:
+            size = shapes[0][0]
+            for start in range(0, groups, size):
+                made.append(Chunk(kind, pl.ds(start, size), pl.ds(0, width)))
+    return made
+
+
+class Traffic:
+    def __init__(self, spot, refs):
+        self.spot = spot
+        self.__dict__.update(refs)
+        self.chunks = chunks_of([tuple(shard.shape) for shard in self.shards])
+
+
+    def own(self, k):
+        chunk, spot = self.chunks[k], self.spot
+        source = self.shards[chunk.kind].at[chunk.groups, :, chunk.cols]
+        target = chunk.block(self.full, spot.layer, spot.seat)
+        for layer in spot.above:
+            remote(
+                source, target, self.sent.at[k], self.along_in.at[k], layer * ROWS + spot.seat
+            ).start()
+
+    def line_out(self, k, seat, device, sem):
+        line = self.chunks[k].line(self.full, seat)
+        remote(line, line, self.sent.at[k], sem, device).start()
+
+    def wait_lines(self, k, sem, count=1):
+        chunk = self.chunks[k]
+        here = chunk.bulk(self.full, 3 if count == 3 else LAYERS, 1 if count == 3 else count)
+        return remote(here, here, self.sent.at[k], sem, self.spot.me)
+
+    def from_line(self, k):
+        spot = self.spot
+        self.wait_lines(k, self.along_in.at[k], 3).wait_recv()
+        self.line_out(k, spot.seat, spot.second, self.second_in.at[k])
+        self.line_out(k, spot.seat, spot.third, self.third_in.at[k, 0])
+        self.line_out(k, spot.seat, spot.sibling, self.sibling_in.at[k])
+
+    def from_second(self, k):
+        spot = self.spot
+        self.wait_lines(k, self.second_in.at[k]).wait_recv()
+        seat = spot.seat + spot.to_second
+        self.line_out(k, seat, spot.third, self.third_in.at[k, 1])
+        self.line_out(k, seat, spot.sibling, self.sibling_in.at[k])
+
+    def from_third(self, k, which):
+        spot = self.spot
+        self.wait_lines(k, self.third_in.at[k, which]).wait_recv()
+        seat = spot.seat + spot.to_third + which * spot.to_second
+        self.line_out(k, seat, spot.sibling, self.sibling_in.at[k])
+
+    def complete(self, k):
+        self.wait_lines(k, self.sibling_in.at[k], 4).wait_recv()
+
+    def own_sent(self, k):
+        self.wait_lines(k, self.sent.at[k], 7).wait_send()
+        self.wait_lines(k, self.sent.at[k], 3).wait_send()
+
+
+    def exchange(self, source, target, which, first=0, last=COUNT - 1):
+        me = self.spot.me
+
+        def go(step, carry):
+            device = lax.rem(me + lax.rem(step * 5, COUNT), COUNT)
+            remote(
+                source.at[:, device],
+                target.at[:, me],
+                self.given.at[which],
+                self.taken.at[which],
+                device,
+            ).start()
+            return carry
+
+        lax.fori_loop(1 + first, 1 + last, go, 0)
+
+    def exchanged(self, target, which):
+        here = target.at[:, pl.ds(0, COUNT - 1)]
+        return remote(
+            here,
+            here,
+            self.given.at[which],
+            self.taken.at[which],
+            self.spot.me,
+        )
+
+    def exchange_small(self, source, target, which):
+        me = self.spot.me
+
+        def go(step, carry):
+            device = lax.rem(me + step, COUNT)
+            remote(
+                source if which == 4 else source.at[device],
+                target.at[me],
+                self.given.at[which],
+                self.taken.at[which],
+                device,
+            ).start()
+            return carry
+
+        lax.fori_loop(1, COUNT, go, 0)
+
+    def exchanged_small(self, target, which):
+        here = target.at[pl.ds(0, COUNT - 1)]
+        return remote(here, here, self.given.at[which], self.taken.at[which], self.spot.me)
+
+
+    def move(self, k, seat, landing, device, sem):
+        remote(
+            self.chunks[k].line(self.partial, seat), landing, self.shed.at[k], sem, device
+        ).start()
+
+    def landing(self, k, landings, slot):
+        chunk = self.chunks[k]
+        return landings[chunk.kind].at[slot, :, chunk.groups, :, chunk.cols]
+
+    def landed(self, k, landings, sem):
+        chunk = self.chunks[k]
+        here = landings[chunk.kind].at[:, :, chunk.groups, :, chunk.cols]
+        remote(here, here, self.shed.at[k], sem, self.spot.me).wait_recv()
+
+    def take_in(self, k, seat, landings, slot):
+        chunk = self.chunks[k]
+        line, here = chunk.line(self.partial, seat), self.landing(k, landings, slot)
+        line[...] = line[...] + here[...]
+
+    def begin(self, k):
+        spot = self.spot
+        for slot in range(4):
+            seat = 2 * slot + (spot.seat + 1) % 2
+            self.move(
+                k, seat, self.landing(k, self.land_first, slot), spot.sibling, self.first_in.at[k]
+            )
+
+    def to_third(self, k):
+        spot = self.spot
+        self.landed(k, self.land_first, self.first_in.at[k])
+        for slot in range(4):
+            self.take_in(k, 2 * slot + spot.seat % 2, self.land_first, slot)
+        for slot in range(2):
+            seat = spot.seat + spot.to_third + slot * spot.to_second
+            self.move(
+                k, seat, self.landing(k, self.land_third, slot), spot.third, self.across_in.at[k]
+            )
+
+    def to_second(self, k):
+        spot = self.spot
+        self.landed(k, self.land_third, self.across_in.at[k])
+        for slot in range(2):
+            self.take_in(k, spot.seat + slot * spot.to_second, self.land_third, slot)
+        seat = spot.seat + spot.to_second
+        self.move(k, seat, self.landing(k, self.land_second, 0), spot.second, self.over_in.at[k])
+
+    def to_owner(self, k):
+        chunk, spot = self.chunks[k], self.spot
+        self.landed(k, self.land_second, self.over_in.at[k])
+        self.take_in(k, spot.seat, self.land_second, 0)
+        target = self.sums[chunk.kind].at[spot.layer, chunk.groups, :, chunk.cols]
+        for layer in spot.above:
+            remote(
+                chunk.block(self.partial, layer, spot.seat),
+                target,
+                self.shed.at[k],
+                self.owner_in.at[k],
+                layer * ROWS + spot.seat,
+            ).start()
+        self.keep(k).start()
+
+    def keep(self, k):
+        chunk, spot = self.chunks[k], self.spot
+        return pltpu.make_async_copy(
+            chunk.block(self.partial, spot.layer, spot.seat),
+            self.sums[chunk.kind].at[spot.layer, chunk.groups, :, chunk.cols],
+            self.kept.at[k],
+        )
+
+    def settle(self, k):
+        chunk = self.chunks[k]
+        here = self.sums[chunk.kind].at[pl.ds(0, 3), chunk.groups, :, chunk.cols]
+        remote(here, here, self.shed.at[k], self.owner_in.at[k], self.spot.me).wait_recv()
+        self.keep(k).wait()
+        for count in (7, 3):
+            there = chunk.bulk(self.partial, 3 if count == 3 else LAYERS, 1 if count == 3 else count)
+            remote(there, there, self.shed.at[k], self.owner_in.at[k], self.spot.me).wait_send()
+
+
+def interleave(count, body, steps=()):
+    assert len(steps) <= count
+
+    def one(index, carry):
+        body(index)
+        for place, thunks in enumerate(steps):
+            if thunks:
+
+                @pl.when(index == place)
+                def _():
+                    for thunk in thunks:
+                        thunk()
+
+        return carry
+
+    lax.fori_loop(0, count, one, 0)
+
+
+def unroll(count, body, steps):
+    for index in range(count):
+        body(index)
+        for thunk in steps[index]:
+            thunk()
+
+
+def spread(thunks, slots):
+    return [
+        thunks[len(thunks) * place // slots : len(thunks) * (place + 1) // slots]
+        for place in range(slots)
+    ]
+
+
+LEAD = 3
+
+
+def step_kernel(trees, *given):
+    given, named = list(given), {}
+    for tree in trees:
+        named.update(jax.tree.unflatten(tree, given[: tree.num_leaves]))
+        given = given[tree.num_leaves :]
+    refs = types.SimpleNamespace(**named)
+    spot = Spot()
+    me = spot.me
+    traffic = Traffic(spot, named)
+    chunks = range(len(traffic.chunks))
+    tokens, cotangent = refs.tokens, refs.cotangent
+    sequence, upstream = refs.sequence, refs.upstream
+    first_spare, second_spare = refs.first_spare, refs.second_spare
+
+    locals_ = [
+        pltpu.make_async_copy(
+            traffic.shards[kind], traffic.full[kind].at[spot.layer, spot.seat], traffic.local.at[kind]
+        )
+        for kind in range(4)
+    ] + [
+        pltpu.make_async_copy(cotangent, first_spare, traffic.local.at[4]),
+        pltpu.make_async_copy(tokens.at[:, me], sequence.at[:, me], traffic.local.at[5]),
+        pltpu.make_async_copy(refs.small_own, refs.small.at[me], traffic.local.at[6]),
+    ]
+    for copy in locals_:
+        copy.start()
+    meet_all(me)
+
+    def tokens_piece(first, last):
+        return lambda: traffic.exchange(tokens, sequence, 0, first, last)
+
+    def piece_of(source, target, which, first, last):
+        return lambda: traffic.exchange(source, target, which, first, last)
+
+    def do(method, *args):
+        return lambda: method(*args)
+
+    layer = Layer(named)
+    layer.context_grad, layer.preact_grad = refs.hidden_low, refs.active
+    layer.result, layer.input_grad = first_spare, second_spare
+    layer.weight_in, layer.weight_mix, layer.weight_up, layer.weight_down = refs.full
+    layer.in_grad, layer.mix_grad, layer.up_grad, layer.down_grad = refs.partial
+    layer.lengths = [refs.lengths[batch, me] for batch in range(2)]
+    tiles, wide = layer.width // TILE, layer.hidden_width // TILE
+    pairs = 2 * (layer.width // PAIR)
+    ins = 3
+    ups = wide // tiles
+    assert len(chunks) == ins + 1 + 2 * ups
+
+    ticks = []
+    token_cuts = [0, 8, 16, 24, COUNT - 1]
+    for tick in range(-LEAD, len(chunks) + 2):
+        here = []
+        if 0 <= tick + LEAD < len(chunks):
+            here.append(do(traffic.own, tick + LEAD))
+        if -LEAD <= tick < 4 - LEAD:
+            here.append(tokens_piece(token_cuts[tick + LEAD], token_cuts[tick + LEAD + 1]))
+        if tick == -LEAD:
+            here.append(do(traffic.exchange_small, refs.small_own, refs.small, 4))
+        if 0 <= tick < len(chunks):
+            here.append(do(traffic.from_line, tick))
+        if 0 <= tick - 1 < len(chunks):
+            here.append(do(traffic.from_second, tick - 1))
+            here.append(do(traffic.from_third, tick - 1, 0))
+        if 0 <= tick - 2 < len(chunks):
+            here.append(do(traffic.from_third, tick - 2, 1))
+        if tick >= 6:
+            first = (tick - 6) * 4
+            if first < COUNT - 1:
+                here.append(
+                    piece_of(second_spare, upstream, 1, first, min(first + 4, COUNT - 1))
+                )
+        ticks.append(here)
+    flat = lambda first, last: [thunk for here in ticks[first + LEAD : last + LEAD] for thunk in here]
+
+    for thunk in flat(-LEAD, 0):
+        thunk()
+    for copy in locals_:
+        copy.wait()
+    layer.terms[...] = jnp.zeros_like(layer.terms)
+    for batch in range(2):
+        for seat in range(COUNT):
+            second_spare[batch, seat] = first_spare[batch, refs.backward_order[batch, seat]]
+    own_upstream = pltpu.make_async_copy(
+        second_spare.at[:, me], upstream.at[:, me], traffic.local.at[7]
+    )
+    own_upstream.start()
+    for thunk in flat(0, 2):
+        thunk()
+    traffic.exchanged_small(refs.small, 4).wait_recv()
+    layer.spread_small()
+    for thunk in flat(2, ins + 2):
+        thunk()
+    traffic.exchanged(sequence, 0).wait_recv()
+    for k in range(ins):
+        traffic.complete(k)
+    interleave(3 * tiles, layer.project, spread(flat(ins + 2, ins + 3), 3 * tiles))
+    interleave(pairs, layer.attend, spread(flat(ins + 3, ins + 6), pairs))
+    traffic.complete(ins)
+    interleave(layer.rows // TILE, layer.mix)
+    for thunk in flat(ins + 6, ins + ups + 3):
+        thunk()
+    for k in range(ins + 1, ins + 1 + ups):
+        traffic.complete(k)
+    interleave(wide, layer.up, spread(flat(ins + ups + 3, len(chunks) + 2), wide))
+    for k in range(ins + 1 + ups, len(chunks)):
+        traffic.complete(k)
+    interleave(tiles, layer.down)
+    own_upstream.wait()
+    cotangents = traffic.exchanged(upstream, 1)
+    cotangents.wait_recv()
+    interleave(layer.rows // 128, layer.finish)
+
+    keep_result = pltpu.make_async_copy(
+        first_spare.at[:, me], refs.returned.at[:, me], traffic.local.at[0]
+    )
+    keep_result.start()
+    pieces = [
+        piece_of(first_spare, refs.returned, 2, first, min(first + 4, COUNT - 1))
+        for first in range(0, COUNT - 1, 4)
+    ]
+    interleave(LAYERS, layer.down_weight_grad, spread(pieces, LAYERS))
+
+    queue = list(range(ins + 1 + ups, len(chunks))) + list(range(ins + 1, ins + 1 + ups))
+    queue += [ins] + list(range(ins))
+    walk = []
+    for tick in range(len(queue) + 2):
+        for late, stage in enumerate((traffic.to_third, traffic.to_second, traffic.to_owner)):
+            if 0 <= tick - late < len(queue):
+                walk.append(do(stage, queue[tick - late]))
+
+    def next_steps(count):
+        taken, walk[:] = walk[:count], walk[count:]
+        return taken
+
+    def with_begin(steps, count, every, kinds):
+        made = [list(step) for step in steps] + [[] for _ in range(count - len(steps))]
+        for place, k in enumerate(kinds):
+            made[(place + 1) * every - 1].insert(0, do(traffic.begin, k))
+        return made
+
+    for k in queue[:ups]:
+        traffic.begin(k)
+    interleave(LAYERS, layer.active_backward, spread(next_steps(3), LAYERS))
+    interleave(
+        wide,
+        layer.up_weight_grad,
+        with_begin(spread(next_steps(3), wide), wide, tiles, queue[ups : 2 * ups]),
+    )
+    unroll(tiles, layer.hidden_backward, spread(next_steps(2), tiles))
+    interleave(layer.rows // 128, layer.first_backward, spread(next_steps(1), 1))
+    interleave(
+        tiles,
+        layer.mix_weight_grad,
+        with_begin(spread(next_steps(1), tiles), tiles, tiles, queue[2 * ups : 2 * ups + 1]),
+    )
+    unroll(tiles, layer.mix_backward, spread(next_steps(1), tiles))
+    interleave(pairs, layer.attend_backward, spread(next_steps(5), pairs))
+    interleave(
+        3 * tiles,
+        layer.in_weight_grad,
+        with_begin(spread(next_steps(3), 3 * tiles), 3 * tiles, tiles, queue[2 * ups + 1 :]),
+    )
+    layer.gather_terms()
+    traffic.exchange_small(refs.small_grad, refs.small_sums, 5)
+    keep_small = pltpu.make_async_copy(
+        refs.small_grad.at[me], refs.small_sums.at[me], traffic.local.at[1]
+    )
+    keep_small.start()
+    cotangents.wait_send()
+    unroll(tiles, layer.input_backward, spread(next_steps(1), tiles))
+    keep_grad = pltpu.make_async_copy(
+        second_spare.at[:, me], refs.tokens_grad.at[:, me], traffic.local.at[2]
+    )
+    keep_grad.start()
+    left = next_steps(len(walk))
+    cuts = list(range(0, COUNT - 1, 4))
+    for place in range(max(len(left), len(cuts))):
+        if place < len(cuts):
+            piece_of(
+                second_spare, refs.tokens_grad, 3, cuts[place], min(cuts[place] + 4, COUNT - 1)
+            )()
+        if place < len(left):
+            left[place]()
+    for k in queue:
+        traffic.settle(k)
+        traffic.own_sent(k)
+    traffic.exchanged(sequence, 0).wait_send()
+    for target, which in ((refs.returned, 2), (refs.tokens_grad, 3)):
+        copy = traffic.exchanged(target, which)
+        copy.wait_recv()
+        copy.wait_send()
+    traffic.exchanged_small(refs.small, 4).wait_send()
+    small = traffic.exchanged_small(refs.small_sums, 5)
+    small.wait_recv()
+    small.wait_send()
+    for copy in (keep_result, keep_small, keep_grad):
+        copy.wait()
+
+
+def encoder_step(lengths, backward_order, tokens, cotangent, shards, small_own):
+    low, full = jnp.bfloat16, jnp.float32
+    width, hidden_width = tokens.shape[-1], shards[2].shape[-1]
+    rows = tokens.shape[0] * COUNT * tokens.shape[2]
+    anywhere = pl.BlockSpec(memory_space=pl.ANY)
+    inputs = dict(
+        lengths=lengths,
+        backward_order=backward_order,
+        tokens=tokens,
+        cotangent=cotangent,
+        shards=shards,
+        small_own=small_own,
+    )
+    shapes = [shard.shape for shard in shards]
+    smalls = ((COUNT,) + small_own.shape, full)
+    outputs = dict(
+        returned=jax.ShapeDtypeStruct(tokens.shape, low),
+        tokens_grad=jax.ShapeDtypeStruct(tokens.shape, low),
+        sums=[jax.ShapeDtypeStruct((LAYERS,) + shape, low) for shape in shapes],
+        small_sums=jax.ShapeDtypeStruct(*smalls),
+    )
+    sequences = pltpu.VMEM(tokens.shape, low)
+    scratch = dict(
+        full=[pltpu.VMEM((LAYERS, ROWS) + shape, low) for shape in shapes],
+        partial=[pltpu.VMEM((LAYERS, ROWS) + shape, low) for shape in shapes],
+        land_first=[pltpu.VMEM((4, LAYERS) + shape, low) for shape in shapes],
+        land_third=[pltpu.VMEM((2, LAYERS) + shape, low) for shape in shapes],
+        land_second=[pltpu.VMEM((1, LAYERS) + shape, low) for shape in shapes],
+        sequence=sequences,
+        upstream=sequences,
+        first_spare=sequences,
+        second_spare=sequences,
+        small=pltpu.VMEM(*smalls),
+        small_grad=pltpu.VMEM(*smalls),
+        **scratch_of(rows, width, hidden_width),
+    )
+    count = len(chunks_of(shapes))
+    each = pltpu.SemaphoreType.DMA((count,))
+    sems = dict(
+        local=pltpu.SemaphoreType.DMA((8,)),
+        given=pltpu.SemaphoreType.DMA((6,)),
+        taken=pltpu.SemaphoreType.DMA((6,)),
+        third_in=pltpu.SemaphoreType.DMA((count, 2)),
+        sent=each,
+        along_in=each,
+        second_in=each,
+        sibling_in=each,
+        shed=each,
+        first_in=each,
+        across_in=each,
+        over_in=each,
+        owner_in=each,
+        kept=each,
+    )
+    smem = pl.BlockSpec(memory_space=pltpu.SMEM)
+    given, given_tree = jax.tree.flatten(inputs)
+    in_specs = [smem if leaf.dtype == jnp.int32 else anywhere for leaf in given]
+    made, made_tree = jax.tree.flatten(outputs)
+    held, held_tree = jax.tree.flatten({**scratch, **sems})
+    results = pl.pallas_call(
+        functools.partial(step_kernel, (given_tree, made_tree, held_tree)),
+        out_shape=made,
+        in_specs=in_specs,
+        out_specs=[anywhere] * len(made),
+        scratch_shapes=held,
+        compiler_params=pltpu.CompilerParams(
+            collective_id=0, has_side_effects=True, vmem_limit_bytes=VMEM_LIMIT
+        ),
+        name="encoder_step",
+    )(*given)
+    results = jax.tree.unflatten(made_tree, results)
+    return types.SimpleNamespace(**results)
+
+
+VMEM_LIMIT = 63 << 20
+
+
+def finish_kernel(order, returned, moved, *refs):
+    sums, small_sums, refs = refs[:4], refs[4], refs[5:]
+    layer_out, tokens_grad, refs = refs[0], refs[1], refs[2:]
+    totals, outs, (sem,) = refs[:4], refs[4:12], refs[12:]
+
+    def deal(step, carry):
+        batch, seat = step // COUNT, step % COUNT
+        pltpu.make_async_copy(
+            returned.at[batch, order[batch, seat]], layer_out.at[batch, seat], sem.at[0]
+        ).start()
+        return carry
+
+    lax.fori_loop(0, 2 * COUNT, deal, 0)
+    copy = pltpu.make_async_copy(moved, tokens_grad, sem.at[1])
+    copy.start()
+    for total, parts in zip(totals, sums):
+        total[...] = sum(parts[layer].astype(jnp.float32) for layer in range(LAYERS))
+    small = jnp.sum(small_sums[...], 0)
+    for place, out in enumerate(outs):
+        out[...] = small[place : place + 1, : out.shape[1]]
+    copy.wait()
+    pltpu.make_async_copy(returned, layer_out, sem.at[0]).wait()
+
+
+def finish_step(order, returned, tokens_grad, sums, small_sums):
+    anywhere = pl.BlockSpec(memory_space=pl.ANY)
+    inside = pl.BlockSpec(memory_space=pltpu.VMEM)
+    return pl.pallas_call(
+        finish_kernel,
+        out_shape=[jax.ShapeDtypeStruct(returned.shape, returned.dtype)] * 2
+        + [jax.ShapeDtypeStruct(part.shape[1:], jnp.float32) for part in sums]
+        + [jax.ShapeDtypeStruct((1, width), jnp.float32) for width in WIDTHS],
+        in_specs=[pl.BlockSpec(memory_space=pltpu.SMEM)] + [anywhere] * 2 + [inside] * 5,
+        out_specs=[anywhere] * 2 + [inside] * 12,
+        scratch_shapes=[pltpu.SemaphoreType.DMA((2,))],
+        name="finish_step",
+    )(order, returned, tokens_grad, *sums, small_sums)
+
+
+SMALL = (1, 3, 4, 5, 7, 9, 10, 11)
+LARGE = (0, 2, 6, 8)
+
+
+def local(tokens, lengths, order, *rest):
+    shards, cotangent = rest[:12], rest[12]
+    if lax.axis_size("dp") != COUNT or tokens.shape[2] % 8:
+        return portable(tokens, lengths, order, *rest)
+    small = sum(
+        lax.pad(
+            shards[i].astype(jnp.float32)[None],
+            jnp.float32(0),
+            ((place, len(SMALL) - 1 - place, 0), (0, 128 - shards[i].shape[0], 0)),
+        )
+        for place, i in enumerate(SMALL)
+    )
+    slots = lax.broadcasted_iota(jnp.int32, order.shape + (COUNT,), 1)
+    targets = lax.broadcasted_iota(jnp.int32, order.shape + (COUNT,), 2)
+    backward_order = jnp.sum(jnp.where(order[:, :, None] == targets, slots, 0), 1)
+    made = encoder_step(
+        lengths,
+        backward_order,
+        tokens,
+        cotangent,
+        [shards[i].reshape(-1, 8, shards[i].shape[-1]) for i in LARGE],
+        small,
+    )
+    layer_out, tokens_grad, *rest = finish_step(
+        order, made.returned, made.tokens_grad, made.sums, made.small_sums
+    )
+    outputs = [None] * 12
+    for i, total in zip(LARGE, rest[:4]):
+        outputs[i] = total.reshape(-1, total.shape[-1])
+    for i, total in zip(SMALL, rest[4:]):
+        outputs[i] = total.reshape(-1)
+    return (layer_out, tokens_grad, *outputs)
+
+
 def solution(mesh):
     return jax.shard_map(
         local,

time: 952 us -> 252 us (0.26); the launches traced: 937 us -> 252 us
  waiting for transfers between devices: 361 us -> 0 us
  matrix products: 280 us -> 0 us
  Pallas kernels: 0 us -> 249 us
  local copies, waits for them, and re-layouts: 94.2 us -> 0.71 us
  blocking collectives: 82.8 us -> 0 us
  other arithmetic: 66.8 us -> 1.26 us
  starting transfers between devices: 31.8 us -> 0 us
  between operations: 19.5 us -> 0.9 us
    dot_general x192 -> x0, matrix products: 280 us -> none  [the longest x56 99.4 us: rows_product(): lax.dot_general(left, right, (((0,), (0,)), ((), ())), preferred_element_...]
    reduce_scatter x4 -> x0, waiting for transfers between devices: 273 us -> none  [the longest x1 142 us: local(): lax.psum_scatter(totals[8], 'dp', scatter_dimension=0, tiled=True)]
    pallas_call x0 -> x2, Pallas kernels: none -> 249 us  [the longest x1 198 us: encoder_step(): pl.pallas_call(functools.partial(step_kernel, (given_tree, made_tree, hel...]
    unnamed x2 -> x0, blocking collectives: 82.8 us -> none
    all_to_all x8 -> x0, waiting for transfers between devices: 49.8 us -> none  [the longest x2 28.8 us: local(): lax.all_to_all(cotangent[batch], 'dp', split_axis=0, concat_axis=1, tiled...]
    all_gather x4 -> x0, waiting for transfers between devices: 35.4 us -> none  [the longest x1 35.4 us: fetch_weights(): lax.all_gather(shards[8], 'dp', axis=0, tiled=True)]
    lt x48 -> x0, other arithmetic: 31.3 us -> none  [forward(): valid = jnp.arange(sequence.shape[0], dtype=jnp.int32) < length]
    unnamed x177 -> x18, local copies, waits for them, and re-layouts: 31.6 us -> 0.71 us
  transfers between devices with their start and end apart: 16 -> 0, of which waited for: 8 -> 0; matrix products, arithmetic and copies ran while one was open for 31% -> 0% of each run, Pallas kernels for 0% -> 0%
where the time goes in v1:
time: 252 us
  Pallas kernels  249 us (99%)
    pallas_call x1, Pallas kernels, encoder_step(): pl.pallas_call(functools.partial(step_kernel, (given_tree, made_tree, hel...  198 us
    pallas_call x1, Pallas kernels, finish_step(): pl.pallas_call(finish_kernel, out_shape=[jax.ShapeDtypeStruct(returned.sh...  51.2 us

profile of v1, /device:TPU:0, one launch (start us, length us, event | category | flops | bytes accessed | tf_op | source)
XLA Modules:
  0.0 252.0 jit_solution(1868904882685321975)
XLA Ops:
  0.6 0.0 copy-start.6
  0.7 0.0 copy-start.7
  0.7 0.0 copy-start.8
  0.7 0.0 copy-start
  0.7 0.0 copy-start.5
  0.7 0.7 copy-done
  1.4 0.0 copy-start.1
  1.4 0.0 copy-start.2
  1.4 0.0 copy-start.3
  1.4 0.0 copy-start.4
  1.4 0.7 select_reduce_fusion.given_0_
  2.0 0.0 copy-done.6
  2.0 0.0 copy-done.7
  2.0 0.0 copy-done.8
  2.0 0.0 copy-done.5
  2.1 0.0 copy-done.1
  2.1 0.0 copy-done.2
  2.1 0.0 copy-done.3
  2.1 0.0 copy-done.4
  2.1 0.6 convert_add_fusion.given_7_
  2.7 197.9 %encoder_step.1 = (bf16[2,32,8,768]{3,2,1,0:T(8,128)(2,1)}, f32[32,8,128]{2,1,0:T(8,128)}, bf16[4,3,8,2304]{3,2,1,0:T(8,128)(2,1)}, bf16[4,3,8,768]{3,2,1,0:T(8,...) custom-call(s32[2,32]{1,0:T(2,128)} %select_reduce_fusion.given_0_, ...), custom_call_target="tpu_custom_call" | custom-call | tf_op jit(solution)/shard_map/encoder_step/pallas_call | solution.py:1238
  200.6 51.2 %finish_step.1 = (bf16[2,32,8,768]{3,2,1,0:T(8,128)(2,1)}, bf16[2,32,8,768]{3,2,1,0:T(8,128)(2,1)}, f32[3,8,2304]{2,1,0:T(8,128)}, f32[3,8,768]{2,1,0:T(8,128)},...) custom-call(s32[2,32]{1,0:T(2,128)} %order.1, ...), custom_call_target="tpu_custom_call" | custom-call | tf_op jit(solution)/shard_map/finish_step/pallas_call | solution.py:1283
Async XLA Ops:
  0.6 1.4 copy-start.6
  0.7 1.4 copy-start.7
  0.7 1.4 copy-start.8
  0.7 0.7 copy-start
  0.7 1.4 copy-start.5
  1.4 0.7 copy-start.1
  1.4 0.7 copy-start.2
  1.4 0.7 copy-start.3
  1.4 0.7 copy-start.4

commit v2 on v1

--- a/solution.py
+++ b/solution.py
@@ -973,7 +973,7 @@
     ]
 
 
-LEAD = 3
+LEAD, TOKENS_EACH, COTANGENT_FROM, COTANGENT_EACH = 1, 6, 5, 5
 
 
 def step_kernel(trees, *given):
@@ -1004,9 +1004,6 @@
         copy.start()
     meet_all(me)
 
-    def tokens_piece(first, last):
-        return lambda: traffic.exchange(tokens, sequence, 0, first, last)
-
     def piece_of(source, target, which, first, last):
         return lambda: traffic.exchange(source, target, which, first, last)
 
@@ -1026,13 +1023,14 @@
     assert len(chunks) == ins + 1 + 2 * ups
 
     ticks = []
-    token_cuts = [0, 8, 16, 24, COUNT - 1]
     for tick in range(-LEAD, len(chunks) + 2):
         here = []
         if 0 <= tick + LEAD < len(chunks):
             here.append(do(traffic.own, tick + LEAD))
-        if -LEAD <= tick < 4 - LEAD:
-            here.append(tokens_piece(token_cuts[tick + LEAD], token_cuts[tick + LEAD + 1]))
+        first = (tick + LEAD) * TOKENS_EACH
+        if first < COUNT - 1:
+            last = min(first + TOKENS_EACH, COUNT - 1)
+            here.append(piece_of(tokens, sequence, 0, first, last))
         if tick == -LEAD:
             here.append(do(traffic.exchange_small, refs.small_own, refs.small, 4))
         if 0 <= tick < len(chunks):
@@ -1042,12 +1040,10 @@
             here.append(do(traffic.from_third, tick - 1, 0))
         if 0 <= tick - 2 < len(chunks):
             here.append(do(traffic.from_third, tick - 2, 1))
-        if tick >= 6:
-            first = (tick - 6) * 4
-            if first < COUNT - 1:
-                here.append(
-                    piece_of(second_spare, upstream, 1, first, min(first + 4, COUNT - 1))
-                )
+        first = (tick - COTANGENT_FROM) * COTANGENT_EACH
+        if 0 <= first < COUNT - 1:
+            last = min(first + COTANGENT_EACH, COUNT - 1)
+            here.append(piece_of(second_spare, upstream, 1, first, last))
         ticks.append(here)
     flat = lambda first, last: [thunk for here in ticks[first + LEAD : last + LEAD] for thunk in here]
 
@@ -1253,43 +1249,47 @@
 VMEM_LIMIT = 63 << 20
 
 
-def finish_kernel(order, returned, moved, *refs):
-    sums, small_sums, refs = refs[:4], refs[4], refs[5:]
+def finish_kernel(order, *refs):
+    sources, refs = refs[:7], refs[7:]
     layer_out, tokens_grad, refs = refs[0], refs[1], refs[2:]
-    totals, outs, (sem,) = refs[:4], refs[4:12], refs[12:]
-
-    def deal(step, carry):
-        batch, seat = step // COUNT, step % COUNT
-        pltpu.make_async_copy(
-            returned.at[batch, order[batch, seat]], layer_out.at[batch, seat], sem.at[0]
-        ).start()
-        return carry
-
-    lax.fori_loop(0, 2 * COUNT, deal, 0)
-    copy = pltpu.make_async_copy(moved, tokens_grad, sem.at[1])
-    copy.start()
-    for total, parts in zip(totals, sums):
+    totals, outs, inner, sems = refs[:4], refs[4:12], refs[12:19], refs[19]
+    copies = [
+        pltpu.make_async_copy(source, target, sems.at[place])
+        for place, (source, target) in enumerate(zip(sources, inner))
+    ]
+    for copy in copies:
+        copy.start()
+    copies[0].wait()
+    for batch in range(2):
+        for seat in range(COUNT):
+            layer_out[batch, seat] = inner[0][batch, order[batch, seat]]
+    copies[1].wait()
+    tokens_grad[...] = inner[1][...]
+    for total, parts, copy in zip(totals, inner[2:6], copies[2:6]):
+        copy.wait()
         total[...] = sum(parts[layer].astype(jnp.float32) for layer in range(LAYERS))
-    small = jnp.sum(small_sums[...], 0)
+    copies[6].wait()
+    small = jnp.sum(inner[6][...], 0)
     for place, out in enumerate(outs):
         out[...] = small[place : place + 1, : out.shape[1]]
-    copy.wait()
-    pltpu.make_async_copy(returned, layer_out, sem.at[0]).wait()
 
 
 def finish_step(order, returned, tokens_grad, sums, small_sums):
-    anywhere = pl.BlockSpec(memory_space=pl.ANY)
     inside = pl.BlockSpec(memory_space=pltpu.VMEM)
+    parts = [returned, tokens_grad, *sums, small_sums]
     return pl.pallas_call(
         finish_kernel,
         out_shape=[jax.ShapeDtypeStruct(returned.shape, returned.dtype)] * 2
         + [jax.ShapeDtypeStruct(part.shape[1:], jnp.float32) for part in sums]
         + [jax.ShapeDtypeStruct((1, width), jnp.float32) for width in WIDTHS],
-        in_specs=[pl.BlockSpec(memory_space=pltpu.SMEM)] + [anywhere] * 2 + [inside] * 5,
-        out_specs=[anywhere] * 2 + [inside] * 12,
-        scratch_shapes=[pltpu.SemaphoreType.DMA((2,))],
+        in_specs=[pl.BlockSpec(memory_space=pltpu.SMEM)]
+        + [pl.BlockSpec(memory_space=pltpu.HBM)] * 7,
+        out_specs=[inside] * 14,
+        scratch_shapes=[pltpu.VMEM(part.shape, part.dtype) for part in parts]
+        + [pltpu.SemaphoreType.DMA((7,))],
+        compiler_params=pltpu.CompilerParams(vmem_limit_bytes=VMEM_LIMIT),
         name="finish_step",
-    )(order, returned, tokens_grad, *sums, small_sums)
+    )(order, *parts)
 
 
 SMALL = (1, 3, 4, 5, 7, 9, 10, 11)

time: 252 us -> 202 us (0.80)
  Pallas kernels: 249 us -> 199 us
    pallas_call x1, Pallas kernels: 51.2 us -> 4.17 us  [finish_step(): pl.pallas_call(finish_kernel, out_shape=[jax.ShapeDtypeStruct(returned.sh...]
    pallas_call x1, Pallas kernels: 198 us -> 195 us  [encoder_step(): pl.pallas_call(functools.partial(step_kernel, (given_tree, made_tree, hel...]
where the time goes in v2:
time: 202 us
  Pallas kernels  199 us (99%)
    pallas_call x1, Pallas kernels, encoder_step(): pl.pallas_call(functools.partial(step_kernel, (given_tree, made_tree, hel...  195 us
    pallas_call x1, Pallas kernels, finish_step(): pl.pallas_call(finish_kernel, out_shape=[jax.ShapeDtypeStruct(returned.sh...  4.17 us

profile of v2, /device:TPU:0, one launch (start us, length us, event | category | flops | bytes accessed | tf_op | source)
XLA Modules:
  0.0 201.6 jit_solution(1330222686422949335)
XLA Ops:
  0.6 0.0 copy-start.6
  0.7 0.0 copy-start.7
  0.7 0.0 copy-start.8
  0.7 0.0 copy-start
  0.7 0.0 copy-start.5
  0.7 0.7 copy-done
  1.4 0.0 copy-start.1
  1.4 0.0 copy-start.2
  1.4 0.0 copy-start.3
  1.4 0.0 copy-start.4
  1.4 0.7 select_reduce_fusion.given_0_
  2.0 0.0 copy-done.6
  2.0 0.0 copy-done.7
  2.0 0.0 copy-done.8
  2.0 0.0 copy-done.5
  2.1 0.0 copy-done.1
  2.1 0.0 copy-done.2
  2.1 0.0 copy-done.3
  2.1 0.0 copy-done.4
  2.1 0.6 convert_add_fusion.given_7_
  2.7 194.6 %encoder_step.1 = (bf16[2,32,8,768]{3,2,1,0:T(8,128)(2,1)}, f32[32,8,128]{2,1,0:T(8,128)}, bf16[4,3,8,2304]{3,2,1,0:T(8,128)(2,1)}, bf16[4,3,8,768]{3,2,1,0:T(8,...) custom-call(s32[2,32]{1,0:T(2,128)} %select_reduce_fusion.given_0_, ...), custom_call_target="tpu_custom_call" | custom-call | tf_op jit(solution)/shard_map/encoder_step/pallas_call | solution.py:1234
  197.3 4.2 %finish_step.1 = (bf16[2,32,8,768]{3,2,1,0:T(8,128)(2,1)}, bf16[2,32,8,768]{3,2,1,0:T(8,128)(2,1)}, f32[3,8,2304]{2,1,0:T(8,128)}, f32[3,8,768]{2,1,0:T(8,128)},...) custom-call(s32[2,32]{1,0:T(2,128)} %order.1, ...), custom_call_target="tpu_custom_call" | custom-call | tf_op jit(solution)/shard_map/finish_step/pallas_call | solution.py:1280
Async XLA Ops:
  0.6 1.4 copy-start.6
  0.7 1.4 copy-start.7
  0.7 1.4 copy-start.8
  0.7 0.7 copy-start
  0.7 1.4 copy-start.5
  1.4 0.7 copy-start.1
  1.4 0.7 copy-start.2
  1.4 0.7 copy-start.3
  1.4 0.7 copy-start.4

commit v3 on v2

--- a/solution.py
+++ b/solution.py
@@ -777,6 +777,8 @@
             remote(
                 source, target, self.sent.at[k], self.along_in.at[k], layer * ROWS + spot.seat
             ).start()
+        remote(source, target, self.sent.at[k], self.second_own.at[k], spot.second).start()
+        remote(source, target, self.sent.at[k], self.third_own.at[k], spot.third).start()
 
     def line_out(self, k, seat, device, sem):
         line = self.chunks[k].line(self.full, seat)
@@ -784,26 +786,33 @@
 
     def wait_lines(self, k, sem, count=1):
         chunk = self.chunks[k]
-        here = chunk.bulk(self.full, 3 if count == 3 else LAYERS, 1 if count == 3 else count)
+        layers = {0: 1, 3: 3}.get(count, LAYERS)
+        here = chunk.bulk(self.full, layers, count if layers == LAYERS else 1)
         return remote(here, here, self.sent.at[k], sem, self.spot.me)
 
     def from_line(self, k):
         spot = self.spot
         self.wait_lines(k, self.along_in.at[k], 3).wait_recv()
-        self.line_out(k, spot.seat, spot.second, self.second_in.at[k])
-        self.line_out(k, spot.seat, spot.third, self.third_in.at[k, 0])
+        for layer in spot.above:
+            block = self.chunks[k].block(self.full, layer, spot.seat)
+            sent = self.sent.at[k]
+            remote(block, block, sent, self.second_in.at[k], spot.second).start()
+            remote(block, block, sent, self.third_in.at[k, 0], spot.third).start()
         self.line_out(k, spot.seat, spot.sibling, self.sibling_in.at[k])
 
     def from_second(self, k):
         spot = self.spot
-        self.wait_lines(k, self.second_in.at[k]).wait_recv()
+        self.wait_lines(k, self.second_own.at[k], 0).wait_recv()
+        self.wait_lines(k, self.second_in.at[k], 3).wait_recv()
         seat = spot.seat + spot.to_second
         self.line_out(k, seat, spot.third, self.third_in.at[k, 1])
         self.line_out(k, seat, spot.sibling, self.sibling_in.at[k])
 
     def from_third(self, k, which):
         spot = self.spot
-        self.wait_lines(k, self.third_in.at[k, which]).wait_recv()
+        if which == 0:
+            self.wait_lines(k, self.third_own.at[k], 0).wait_recv()
+        self.wait_lines(k, self.third_in.at[k, which], 1 if which else 3).wait_recv()
         seat = spot.seat + spot.to_third + which * spot.to_second
         self.line_out(k, seat, spot.sibling, self.sibling_in.at[k])
 
@@ -973,7 +982,8 @@
     ]
 
 
-LEAD, TOKENS_EACH, COTANGENT_FROM, COTANGENT_EACH = 1, 6, 5, 5
+PACES = 3, 3, 2, 1, 1, 1, 5, 3, 1
+LEAD, TOKENS_EACH, COTANGENT_FROM, COTANGENT_EACH = 1, 6, 4, 4
 
 
 def step_kernel(trees, *given):
@@ -996,12 +1006,25 @@
         )
         for kind in range(4)
     ] + [
-        pltpu.make_async_copy(cotangent, first_spare, traffic.local.at[4]),
-        pltpu.make_async_copy(tokens.at[:, me], sequence.at[:, me], traffic.local.at[5]),
+        pltpu.make_async_copy(cotangent.at[:, me], upstream.at[:, me], traffic.local.at[5]),
         pltpu.make_async_copy(refs.small_own, refs.small.at[me], traffic.local.at[6]),
     ]
-    for copy in locals_:
+    early = [
+        pltpu.make_async_copy(tokens, first_spare, traffic.local.at[4]),
+        pltpu.make_async_copy(refs.lengths, refs.lengths_here, traffic.local.at[7]),
+        pltpu.make_async_copy(refs.order, refs.order_here, traffic.local.at[8]),
+    ]
+    for copy in early + locals_:
         copy.start()
+    for copy in early:
+        copy.wait()
+    for batch in range(2):
+        for seat in range(COUNT):
+            second_spare[batch, seat] = first_spare[batch, refs.order_here[batch, seat]]
+    own_sequence = pltpu.make_async_copy(
+        second_spare.at[:, me], sequence.at[:, me], traffic.local.at[4]
+    )
+    own_sequence.start()
     meet_all(me)
 
     def piece_of(source, target, which, first, last):
@@ -1015,7 +1038,9 @@
     layer.result, layer.input_grad = first_spare, second_spare
     layer.weight_in, layer.weight_mix, layer.weight_up, layer.weight_down = refs.full
     layer.in_grad, layer.mix_grad, layer.up_grad, layer.down_grad = refs.partial
-    layer.lengths = [refs.lengths[batch, me] for batch in range(2)]
+    layer.lengths = [
+        refs.lengths_here[batch, refs.order_here[batch, me]] for batch in range(2)
+    ]
     tiles, wide = layer.width // TILE, layer.hidden_width // TILE
     pairs = 2 * (layer.width // PAIR)
     ins = 3
@@ -1030,7 +1055,7 @@
         first = (tick + LEAD) * TOKENS_EACH
         if first < COUNT - 1:
             last = min(first + TOKENS_EACH, COUNT - 1)
-            here.append(piece_of(tokens, sequence, 0, first, last))
+            here.append(piece_of(second_spare, sequence, 0, first, last))
         if tick == -LEAD:
             here.append(do(traffic.exchange_small, refs.small_own, refs.small, 4))
         if 0 <= tick < len(chunks):
@@ -1043,7 +1068,7 @@
         first = (tick - COTANGENT_FROM) * COTANGENT_EACH
         if 0 <= first < COUNT - 1:
             last = min(first + COTANGENT_EACH, COUNT - 1)
-            here.append(piece_of(second_spare, upstream, 1, first, last))
+            here.append(piece_of(cotangent, upstream, 1, first, last))
         ticks.append(here)
     flat = lambda first, last: [thunk for here in ticks[first + LEAD : last + LEAD] for thunk in here]
 
@@ -1052,20 +1077,15 @@
     for copy in locals_:
         copy.wait()
     layer.terms[...] = jnp.zeros_like(layer.terms)
-    for batch in range(2):
-        for seat in range(COUNT):
-            second_spare[batch, seat] = first_spare[batch, refs.backward_order[batch, seat]]
-    own_upstream = pltpu.make_async_copy(
-        second_spare.at[:, me], upstream.at[:, me], traffic.local.at[7]
-    )
-    own_upstream.start()
     for thunk in flat(0, 2):
         thunk()
     traffic.exchanged_small(refs.small, 4).wait_recv()
     layer.spread_small()
     for thunk in flat(2, ins + 2):
         thunk()
-    traffic.exchanged(sequence, 0).wait_recv()
+    dealt = traffic.exchanged(sequence, 0)
+    dealt.wait_recv()
+    own_sequence.wait()
     for k in range(ins):
         traffic.complete(k)
     interleave(3 * tiles, layer.project, spread(flat(ins + 2, ins + 3), 3 * tiles))
@@ -1080,7 +1100,6 @@
     for k in range(ins + 1 + ups, len(chunks)):
         traffic.complete(k)
     interleave(tiles, layer.down)
-    own_upstream.wait()
     cotangents = traffic.exchanged(upstream, 1)
     cotangents.wait_recv()
     interleave(layer.rows // 128, layer.finish)
@@ -1115,39 +1134,53 @@
 
     for k in queue[:ups]:
         traffic.begin(k)
-    interleave(LAYERS, layer.active_backward, spread(next_steps(3), LAYERS))
+    paces = iter(PACES)
+    interleave(LAYERS, layer.active_backward, spread(next_steps(next(paces)), LAYERS))
     interleave(
         wide,
         layer.up_weight_grad,
-        with_begin(spread(next_steps(3), wide), wide, tiles, queue[ups : 2 * ups]),
-    )
-    unroll(tiles, layer.hidden_backward, spread(next_steps(2), tiles))
-    interleave(layer.rows // 128, layer.first_backward, spread(next_steps(1), 1))
+        with_begin(
+            [[]] * tiles + spread(next_steps(next(paces)), wide - tiles),
+            wide,
+            tiles,
+            queue[ups : 2 * ups],
+        ),
+    )
+    unroll(tiles, layer.hidden_backward, spread(next_steps(next(paces)), tiles))
+    interleave(layer.rows // 128, layer.first_backward, spread(next_steps(next(paces)), 1))
     interleave(
         tiles,
         layer.mix_weight_grad,
-        with_begin(spread(next_steps(1), tiles), tiles, tiles, queue[2 * ups : 2 * ups + 1]),
-    )
-    unroll(tiles, layer.mix_backward, spread(next_steps(1), tiles))
-    interleave(pairs, layer.attend_backward, spread(next_steps(5), pairs))
+        with_begin(
+            spread(next_steps(next(paces)), tiles), tiles, tiles, queue[2 * ups : 2 * ups + 1]
+        ),
+    )
+    unroll(tiles, layer.mix_backward, spread(next_steps(next(paces)), tiles))
+    interleave(pairs, layer.attend_backward, spread(next_steps(next(paces)), pairs))
     interleave(
         3 * tiles,
         layer.in_weight_grad,
-        with_begin(spread(next_steps(3), 3 * tiles), 3 * tiles, tiles, queue[2 * ups + 1 :]),
-    )
-    layer.gather_terms()
-    traffic.exchange_small(refs.small_grad, refs.small_sums, 5)
+        with_begin(
+            spread(next_steps(next(paces)), 3 * tiles), 3 * tiles, tiles, queue[2 * ups + 1 :]
+        ),
+    )
+    dealt.wait_send()
+    unroll(tiles, layer.input_backward, spread(next_steps(next(paces)), tiles))
+    keep_grad = pltpu.make_async_copy(
+        second_spare.at[:, me], refs.tokens_grad.at[:, me], traffic.local.at[2]
+    )
+    keep_grad.start()
+    left = next_steps(len(walk))
+
+    def small_out():
+        layer.gather_terms()
+        traffic.exchange_small(refs.small_grad, refs.small_sums, 5)
+        keep_small.start()
+
     keep_small = pltpu.make_async_copy(
         refs.small_grad.at[me], refs.small_sums.at[me], traffic.local.at[1]
     )
-    keep_small.start()
-    cotangents.wait_send()
-    unroll(tiles, layer.input_backward, spread(next_steps(1), tiles))
-    keep_grad = pltpu.make_async_copy(
-        second_spare.at[:, me], refs.tokens_grad.at[:, me], traffic.local.at[2]
-    )
-    keep_grad.start()
-    left = next_steps(len(walk))
+    left.insert(2, small_out)
     cuts = list(range(0, COUNT - 1, 4))
     for place in range(max(len(left), len(cuts))):
         if place < len(cuts):
@@ -1159,7 +1192,7 @@
     for k in queue:
         traffic.settle(k)
         traffic.own_sent(k)
-    traffic.exchanged(sequence, 0).wait_send()
+    cotangents.wait_send()
     for target, which in ((refs.returned, 2), (refs.tokens_grad, 3)):
         copy = traffic.exchanged(target, which)
         copy.wait_recv()
@@ -1172,14 +1205,14 @@
         copy.wait()
 
 
-def encoder_step(lengths, backward_order, tokens, cotangent, shards, small_own):
+def encoder_step(lengths, order, tokens, cotangent, shards, small_own):
     low, full = jnp.bfloat16, jnp.float32
     width, hidden_width = tokens.shape[-1], shards[2].shape[-1]
     rows = tokens.shape[0] * COUNT * tokens.shape[2]
     anywhere = pl.BlockSpec(memory_space=pl.ANY)
     inputs = dict(
         lengths=lengths,
-        backward_order=backward_order,
+        order=order,
         tokens=tokens,
         cotangent=cotangent,
         shards=shards,
@@ -1204,6 +1237,8 @@
         upstream=sequences,
         first_spare=sequences,
         second_spare=sequences,
+        lengths_here=pltpu.SMEM(lengths.shape, lengths.dtype),
+        order_here=pltpu.SMEM(order.shape, order.dtype),
         small=pltpu.VMEM(*smalls),
         small_grad=pltpu.VMEM(*smalls),
         **scratch_of(rows, width, hidden_width),
@@ -1211,13 +1246,15 @@
     count = len(chunks_of(shapes))
     each = pltpu.SemaphoreType.DMA((count,))
     sems = dict(
-        local=pltpu.SemaphoreType.DMA((8,)),
+        local=pltpu.SemaphoreType.DMA((9,)),
         given=pltpu.SemaphoreType.DMA((6,)),
         taken=pltpu.SemaphoreType.DMA((6,)),
         third_in=pltpu.SemaphoreType.DMA((count, 2)),
         sent=each,
         along_in=each,
         second_in=each,
+        second_own=each,
+        third_own=each,
         sibling_in=each,
         shed=each,
         first_in=each,
@@ -1226,15 +1263,13 @@
         owner_in=each,
         kept=each,
     )
-    smem = pl.BlockSpec(memory_space=pltpu.SMEM)
     given, given_tree = jax.tree.flatten(inputs)
-    in_specs = [smem if leaf.dtype == jnp.int32 else anywhere for leaf in given]
     made, made_tree = jax.tree.flatten(outputs)
     held, held_tree = jax.tree.flatten({**scratch, **sems})
     results = pl.pallas_call(
         functools.partial(step_kernel, (given_tree, made_tree, held_tree)),
         out_shape=made,
-        in_specs=in_specs,
+        in_specs=[anywhere] * len(given),
         out_specs=[anywhere] * len(made),
         scratch_shapes=held,
         compiler_params=pltpu.CompilerParams(
@@ -1255,19 +1290,18 @@
     totals, outs, inner, sems = refs[:4], refs[4:12], refs[12:19], refs[19]
     copies = [
         pltpu.make_async_copy(source, target, sems.at[place])
-        for place, (source, target) in enumerate(zip(sources, inner))
+        for place, (source, target) in enumerate(zip(sources, (layer_out, *inner[1:])))
     ]
     for copy in copies:
         copy.start()
-    copies[0].wait()
+    copies[1].wait()
     for batch in range(2):
-        for seat in range(COUNT):
-            layer_out[batch, seat] = inner[0][batch, order[batch, seat]]
-    copies[1].wait()
-    tokens_grad[...] = inner[1][...]
+        for slot in range(COUNT):
+            tokens_grad[batch, order[batch, slot]] = inner[1][batch, slot]
     for total, parts, copy in zip(totals, inner[2:6], copies[2:6]):
         copy.wait()
         total[...] = sum(parts[layer].astype(jnp.float32) for layer in range(LAYERS))
+    copies[0].wait()
     copies[6].wait()
     small = jnp.sum(inner[6][...], 0)
     for place, out in enumerate(outs):
@@ -1308,12 +1342,9 @@
         )
         for place, i in enumerate(SMALL)
     )
-    slots = lax.broadcasted_iota(jnp.int32, order.shape + (COUNT,), 1)
-    targets = lax.broadcasted_iota(jnp.int32, order.shape + (COUNT,), 2)
-    backward_order = jnp.sum(jnp.where(order[:, :, None] == targets, slots, 0), 1)
     made = encoder_step(
         lengths,
-        backward_order,
+        order,
         tokens,
         cotangent,
         [shards[i].reshape(-1, 8, shards[i].shape[-1]) for i in LARGE],

time: 202 us -> 198 us (0.980)
  Pallas kernels: 199 us -> 196 us
    pallas_call x1, Pallas kernels: 195 us -> 192 us  [encoder_step(): pl.pallas_call(functools.partial(step_kernel, (given_tree, made_tree, hel...]
where the time goes in v3:
time: 198 us
  Pallas kernels  196 us (99%)
    pallas_call x1, Pallas kernels, encoder_step(): pl.pallas_call(functools.partial(step_kernel, (given_tree, made_tree, hel...  192 us
    pallas_call x1, Pallas kernels, finish_step(): pl.pallas_call(finish_kernel, out_shape=[jax.ShapeDtypeStruct(returned.sh...  4.17 us

profile of v3, /device:TPU:0, one launch (start us, length us, event | category | flops | bytes accessed | tf_op | source)
XLA Modules:
  0.0 198.0 jit_solution(13171311431627170633)
XLA Ops:
  0.6 0.0 copy-start.7
  0.7 0.0 copy-start.3
  0.7 0.0 copy-start.4
  0.7 0.0 copy-start.5
  0.7 0.0 copy-start.6
  0.7 0.0 copy-start
  0.7 0.0 copy-start.1
  0.7 0.0 copy-start.2
  0.7 0.6 copy-done.7
  1.3 0.0 copy-done.3
  1.3 0.0 copy-done.4
  1.3 0.0 copy-done.5
  1.4 0.0 copy-done.6
  1.4 0.0 copy-done
  1.4 0.0 copy-done.1
  1.4 0.0 copy-done.2
  1.4 0.6 convert_add_fusion.given_7_
  2.0 191.7 %encoder_step.1 = (bf16[2,32,8,768]{3,2,1,0:T(8,128)(2,1)}, f32[32,8,128]{2,1,0:T(8,128)}, bf16[4,3,8,2304]{3,2,1,0:T(8,128)(2,1)}, bf16[4,3,8,768]{3,2,1,0:T(8,...) custom-call(bf16[2,32,8,768]{3,2,1,0:T(8,128)(2,1)} %given_0_.1, ...), custom_call_target="tpu_custom_call" | custom-call | tf_op jit(solution)/shard_map/encoder_step/pallas_call | solution.py:1269
  193.7 4.2 %finish_step.1 = (bf16[2,32,8,768]{3,2,1,0:T(8,128)(2,1)}, bf16[2,32,8,768]{3,2,1,0:T(8,128)(2,1)}, f32[3,8,2304]{2,1,0:T(8,128)}, f32[3,8,768]{2,1,0:T(8,128)},...) custom-call(s32[2,32]{1,0:T(2,128)} %order.1, ...), custom_call_target="tpu_custom_call" | custom-call | tf_op jit(solution)/shard_map/finish_step/pallas_call | solution.py:1314
Async XLA Ops:
  0.6 0.7 copy-start.7
  0.7 0.7 copy-start.3
  0.7 0.7 copy-start.4
  0.7 0.7 copy-start.5
  0.7 0.7 copy-start.6
  0.7 0.7 copy-start
  0.7 0.7 copy-start.1
  0.7 0.7 copy-start.2

commit v4 on v3

--- a/solution.py
+++ b/solution.py
@@ -880,15 +880,62 @@
         chunk = self.chunks[k]
         return landings[chunk.kind].at[slot, :, chunk.groups, :, chunk.cols]
 
-    def landed(self, k, landings, sem):
+    def landed(self, k, landings, sem, layers=LAYERS):
         chunk = self.chunks[k]
-        here = landings[chunk.kind].at[:, :, chunk.groups, :, chunk.cols]
+        here = landings[chunk.kind].at[:, pl.ds(0, layers), chunk.groups, :, chunk.cols]
         remote(here, here, self.shed.at[k], sem, self.spot.me).wait_recv()
 
     def take_in(self, k, seat, landings, slot):
         chunk = self.chunks[k]
         line, here = chunk.line(self.partial, seat), self.landing(k, landings, slot)
         line[...] = line[...] + here[...]
+
+
+    def move_block(self, k, layer, seat, landings, slot, device, sem):
+        chunk = self.chunks[k]
+        remote(
+            chunk.block(self.partial, layer, seat),
+            landings[chunk.kind].at[slot, layer, chunk.groups, :, chunk.cols],
+            self.shed.at[k],
+            sem,
+            device,
+        ).start()
+
+    def take_block(self, k, layer, seat, landings, slot):
+        chunk = self.chunks[k]
+        block = chunk.block(self.partial, layer, seat)
+        here = landings[chunk.kind].at[slot, layer, chunk.groups, :, chunk.cols]
+        block[...] = block[...] + here[...]
+
+    def blocks_to_third(self, k, layers, sem):
+        spot = self.spot
+        for layer in layers:
+            for slot in range(2):
+                seat = spot.seat + spot.to_third + slot * spot.to_second
+                self.move_block(k, layer, seat, self.land_third, slot, spot.third, sem)
+
+    def blocks_to_second(self, k, layers, sem, next_sem):
+        spot = self.spot
+        self.landed(k, self.land_third, sem, len(layers))
+        for layer in layers:
+            for slot in range(2):
+                seat = spot.seat + slot * spot.to_second
+                self.take_block(k, layer, seat, self.land_third, slot)
+            seat = spot.seat + spot.to_second
+            self.move_block(k, layer, seat, self.land_second, 0, spot.second, next_sem)
+
+    def late_third(self, k):
+        self.blocks_to_third(k, [self.spot.layer], self.across_own.at[k])
+
+    def late_second(self, k):
+        self.blocks_to_second(
+            k, [self.spot.layer], self.across_own.at[k], self.over_own.at[k]
+        )
+
+    def late_owner(self, k):
+        self.landed(k, self.land_second, self.over_own.at[k], 1)
+        self.take_block(k, self.spot.layer, self.spot.seat, self.land_second, 0)
+        self.keep(k).start()
 
     def begin(self, k):
         spot = self.spot
@@ -903,6 +950,9 @@
         self.landed(k, self.land_first, self.first_in.at[k])
         for slot in range(4):
             self.take_in(k, 2 * slot + spot.seat % 2, self.land_first, slot)
+        if k in self.late:
+            self.blocks_to_third(k, spot.above, self.across_in.at[k])
+            return
         for slot in range(2):
             seat = spot.seat + spot.to_third + slot * spot.to_second
             self.move(
@@ -911,6 +961,9 @@
 
     def to_second(self, k):
         spot = self.spot
+        if k in self.late:
+            self.blocks_to_second(k, spot.above, self.across_in.at[k], self.over_in.at[k])
+            return
         self.landed(k, self.land_third, self.across_in.at[k])
         for slot in range(2):
             self.take_in(k, spot.seat + slot * spot.to_second, self.land_third, slot)
@@ -919,8 +972,13 @@
 
     def to_owner(self, k):
         chunk, spot = self.chunks[k], self.spot
-        self.landed(k, self.land_second, self.over_in.at[k])
-        self.take_in(k, spot.seat, self.land_second, 0)
+        if k in self.late:
+            self.landed(k, self.land_second, self.over_in.at[k], 3)
+            for layer in spot.above:
+                self.take_block(k, layer, spot.seat, self.land_second, 0)
+        else:
+            self.landed(k, self.land_second, self.over_in.at[k])
+            self.take_in(k, spot.seat, self.land_second, 0)
         target = self.sums[chunk.kind].at[spot.layer, chunk.groups, :, chunk.cols]
         for layer in spot.above:
             remote(
@@ -930,7 +988,8 @@
                 self.owner_in.at[k],
                 layer * ROWS + spot.seat,
             ).start()
-        self.keep(k).start()
+        if k not in self.late:
+            self.keep(k).start()
 
     def keep(self, k):
         chunk, spot = self.chunks[k], self.spot
@@ -982,7 +1041,8 @@
     ]
 
 
-PACES = 3, 3, 2, 1, 1, 1, 5, 3, 1
+LATE = 11
+PACES = 3, 3, 3, 0, 1, 2, 6, 3, 1
 LEAD, TOKENS_EACH, COTANGENT_FROM, COTANGENT_EACH = 1, 6, 4, 4
 
 
@@ -1116,11 +1176,16 @@
 
     queue = list(range(ins + 1 + ups, len(chunks))) + list(range(ins + 1, ins + 1 + ups))
     queue += [ins] + list(range(ins))
+    traffic.late = queue[len(queue) - LATE :]
     walk = []
     for tick in range(len(queue) + 2):
         for late, stage in enumerate((traffic.to_third, traffic.to_second, traffic.to_owner)):
             if 0 <= tick - late < len(queue):
                 walk.append(do(stage, queue[tick - late]))
+        if tick == len(queue) - 1:
+            walk += [do(traffic.late_third, k) for k in traffic.late]
+    for stage in (traffic.late_second, traffic.late_owner):
+        walk += [do(stage, k) for k in traffic.late]
 
     def next_steps(count):
         taken, walk[:] = walk[:count], walk[count:]
@@ -1260,6 +1325,8 @@
         first_in=each,
         across_in=each,
         over_in=each,
+        across_own=each,
+        over_own=each,
         owner_in=each,
         kept=each,
     )
@@ -1285,42 +1352,54 @@
 
 
 def finish_kernel(order, *refs):
-    sources, refs = refs[:7], refs[7:]
-    layer_out, tokens_grad, refs = refs[0], refs[1], refs[2:]
-    totals, outs, inner, sems = refs[:4], refs[4:12], refs[12:19], refs[19]
+    sources, targets, inner, ready = refs[:7], refs[7:21], refs[21:28], refs[28:42]
+    sems, out_sems = refs[42:]
     copies = [
         pltpu.make_async_copy(source, target, sems.at[place])
-        for place, (source, target) in enumerate(zip(sources, (layer_out, *inner[1:])))
+        for place, (source, target) in enumerate(zip(sources, (ready[0], *inner[1:])))
     ]
-    for copy in copies:
-        copy.start()
+    outward = [
+        pltpu.make_async_copy(source, target, out_sems.at[place])
+        for place, (source, target) in enumerate(zip(ready, targets))
+    ]
+    for place in (1, 0, 6, 2, 3, 4, 5):
+        copies[place].start()
     copies[1].wait()
     for batch in range(2):
         for slot in range(COUNT):
-            tokens_grad[batch, order[batch, slot]] = inner[1][batch, slot]
-    for total, parts, copy in zip(totals, inner[2:6], copies[2:6]):
-        copy.wait()
-        total[...] = sum(parts[layer].astype(jnp.float32) for layer in range(LAYERS))
+            ready[1][batch, order[batch, slot]] = inner[1][batch, slot]
+    outward[1].start()
     copies[0].wait()
+    outward[0].start()
     copies[6].wait()
     small = jnp.sum(inner[6][...], 0)
-    for place, out in enumerate(outs):
+    for place, out in enumerate(ready[6:]):
         out[...] = small[place : place + 1, : out.shape[1]]
+        outward[6 + place].start()
+    for place in (2, 3, 4, 5):
+        copies[place].wait()
+        parts = inner[place]
+        ready[place][...] = sum(parts[layer].astype(jnp.float32) for layer in range(LAYERS))
+        outward[place].start()
+    for copy in outward:
+        copy.wait()
 
 
 def finish_step(order, returned, tokens_grad, sums, small_sums):
-    inside = pl.BlockSpec(memory_space=pltpu.VMEM)
+    outside = pl.BlockSpec(memory_space=pltpu.HBM)
     parts = [returned, tokens_grad, *sums, small_sums]
+    made = (
+        [jax.ShapeDtypeStruct(returned.shape, returned.dtype)] * 2
+        + [jax.ShapeDtypeStruct(part.shape[1:], jnp.float32) for part in sums]
+        + [jax.ShapeDtypeStruct((1, width), jnp.float32) for width in WIDTHS]
+    )
     return pl.pallas_call(
         finish_kernel,
-        out_shape=[jax.ShapeDtypeStruct(returned.shape, returned.dtype)] * 2
-        + [jax.ShapeDtypeStruct(part.shape[1:], jnp.float32) for part in sums]
-        + [jax.ShapeDtypeStruct((1, width), jnp.float32) for width in WIDTHS],
-        in_specs=[pl.BlockSpec(memory_space=pltpu.SMEM)]
-        + [pl.BlockSpec(memory_space=pltpu.HBM)] * 7,
-        out_specs=[inside] * 14,
-        scratch_shapes=[pltpu.VMEM(part.shape, part.dtype) for part in parts]
-        + [pltpu.SemaphoreType.DMA((7,))],
+        out_shape=made,
+        in_specs=[pl.BlockSpec(memory_space=pltpu.SMEM)] + [outside] * len(parts),
+        out_specs=[outside] * len(made),
+        scratch_shapes=[pltpu.VMEM(part.shape, part.dtype) for part in parts + made]
+        + [pltpu.SemaphoreType.DMA((len(parts),)), pltpu.SemaphoreType.DMA((len(made),))],
         compiler_params=pltpu.CompilerParams(vmem_limit_bytes=VMEM_LIMIT),
         name="finish_step",
     )(order, *parts)

time: 198 us -> 195 us (0.985)
  Pallas kernels: 196 us -> 193 us
    pallas_call x1, Pallas kernels: 192 us -> 189 us  [encoder_step(): pl.pallas_call(functools.partial(step_kernel, (given_tree, made_tree, hel...]
where the time goes in v4:
time: 195 us
  Pallas kernels  193 us (99%)
    pallas_call x1, Pallas kernels, encoder_step(): pl.pallas_call(functools.partial(step_kernel, (given_tree, made_tree, hel...  189 us

profile of v4, /device:TPU:0, one launch (start us, length us, event | category | flops | bytes accessed | tf_op | source)
XLA Modules:
  0.0 194.9 jit_solution(7758353541485531469)
XLA Ops:
  0.6 0.0 copy-start.7
  0.7 0.0 copy-start.3
  0.7 0.0 copy-start.4
  0.7 0.0 copy-start.5
  0.7 0.0 copy-start.6
  0.7 0.0 copy-start
  0.7 0.0 copy-start.1
  0.7 0.0 copy-start.2
  0.7 0.6 copy-done.7
  1.3 0.0 copy-done.3
  1.3 0.0 copy-done.4
  1.3 0.0 copy-done.5
  1.4 0.0 copy-done.6
  1.4 0.0 copy-done
  1.4 0.0 copy-done.1
  1.4 0.0 copy-done.2
  1.4 0.6 convert_add_fusion.given_7_
  2.0 189.1 %encoder_step.1 = (bf16[2,32,8,768]{3,2,1,0:T(8,128)(2,1)}, f32[32,8,128]{2,1,0:T(8,128)}, bf16[4,3,8,2304]{3,2,1,0:T(8,128)(2,1)}, bf16[4,3,8,768]{3,2,1,0:T(8,...) custom-call(bf16[2,32,8,768]{3,2,1,0:T(8,128)(2,1)} %given_0_.1, ...), custom_call_target="tpu_custom_call" | custom-call | tf_op jit(solution)/shard_map/encoder_step/pallas_call | solution.py:1336
  191.1 3.6 %finish_step.1 = (bf16[2,32,8,768]{3,2,1,0:T(8,128)(2,1)}, bf16[2,32,8,768]{3,2,1,0:T(8,128)(2,1)}, f32[3,8,2304]{2,1,0:T(8,128)}, f32[3,8,768]{2,1,0:T(8,128)},...) custom-call(s32[2,32]{1,0:T(2,128)} %order.1, ...), custom_call_target="tpu_custom_call" | custom-call | tf_op jit(solution)/shard_map/finish_step/pallas_call | solution.py:1396
Async XLA Ops:
  0.6 0.7 copy-start.7
  0.7 0.7 copy-start.3
  0.7 0.7 copy-start.4
  0.7 0.7 copy-start.5
  0.7 0.7 copy-start.6
  0.7 0.7 copy-start
  0.7 0.7 copy-start.1
  0.7 0.7 copy-start.2

commit v5 on v4

--- a/solution.py
+++ b/solution.py
@@ -1169,8 +1169,8 @@
     )
     keep_result.start()
     pieces = [
-        piece_of(first_spare, refs.returned, 2, first, min(first + 4, COUNT - 1))
-        for first in range(0, COUNT - 1, 4)
+        piece_of(first_spare, refs.returned, 2, first, min(first + 8, COUNT - 1))
+        for first in range(0, COUNT - 1, 8)
     ]
     interleave(LAYERS, layer.down_weight_grad, spread(pieces, LAYERS))
 

time: 195 us -> 195 us (level)
  no operation moved by 1% of the time
where the time goes in v5:
time: 195 us
  Pallas kernels  193 us (99%)
    pallas_call x1, Pallas kernels, encoder_step(): pl.pallas_call(functools.partial(step_kernel, (given_tree, made_tree, hel...  189 us

profile of v5, /device:TPU:0, one launch (start us, length us, event | category | flops | bytes accessed | tf_op | source)
XLA Modules:
  0.0 194.9 jit_solution(7807622507169822315)
XLA Ops:
  0.6 0.0 copy-start.7
  0.7 0.0 copy-start.3
  0.7 0.0 copy-start.4
  0.7 0.0 copy-start.5
  0.7 0.0 copy-start.6
  0.7 0.0 copy-start
  0.7 0.0 copy-start.1
  0.7 0.0 copy-start.2
  0.7 0.6 copy-done.7
  1.3 0.0 copy-done.3
  1.3 0.0 copy-done.4
  1.3 0.0 copy-done.5
  1.4 0.0 copy-done.6
  1.4 0.0 copy-done
  1.4 0.0 copy-done.1
  1.4 0.0 copy-done.2
  1.4 0.6 convert_add_fusion.given_7_
  2.0 189.1 %encoder_step.1 = (bf16[2,32,8,768]{3,2,1,0:T(8,128)(2,1)}, f32[32,8,128]{2,1,0:T(8,128)}, bf16[4,3,8,2304]{3,2,1,0:T(8,128)(2,1)}, bf16[4,3,8,768]{3,2,1,0:T(8,...) custom-call(bf16[2,32,8,768]{3,2,1,0:T(8,128)(2,1)} %given_0_.1, ...), custom_call_target="tpu_custom_call" | custom-call | tf_op jit(solution)/shard_map/encoder_step/pallas_call | solution.py:1336
  191.1 3.6 %finish_step.1 = (bf16[2,32,8,768]{3,2,1,0:T(8,128)(2,1)}, bf16[2,32,8,768]{3,2,1,0:T(8,128)(2,1)}, f32[3,8,2304]{2,1,0:T(8,128)}, f32[3,8,768]{2,1,0:T(8,128)},...) custom-call(s32[2,32]{1,0:T(2,128)} %order.1, ...), custom_call_target="tpu_custom_call" | custom-call | tf_op jit(solution)/shard_map/finish_step/pallas_call | solution.py:1396
Async XLA Ops:
  0.6 0.7 copy-start.7
  0.7 0.7 copy-start.3
  0.7 0.7 copy-start.4
  0.7 0.7 copy-start.5
  0.7 0.7 copy-start.6
  0.7 0.7 copy-start
  0.7 0.7 copy-start.1
  0.7 0.7 copy-start.2
